TPU v7x, 32 devices: a whole 2x2x4 slice. The times are simulated.
32 devices in a mesh: shard: 8 (over y, x, core), expert: 4 (over z).
Axes of the slice: x: 2, y: 2, z: 4, core: 2. Of those that a mesh axis runs over, the one named last changes fastest.
Arguments:
- tokens: bfloat16 [2, 4, 1024, 1024], P(None, 'expert', 'shard'), may hold values from -6 to 6
- segments: int32 [2, 4, 1024], P(None, 'expert'), may hold values from 0 to 3, never falling along the last dimension, each value on 1 to 512 neighbouring positions
- routes: int32 [2, 4, 1024, 1], P(None, 'expert', 'shard'), may hold values from 0 to 7; in each aligned block of 128 rows (0 to 127, 128 to 255, ..., all dimensions but the last counted through in order) at most 32 rows name the same one
- cotangent: bfloat16 [2, 4, 1024, 1024], P(None, 'expert', 'shard'), may hold values from -6 to 6
- norm1_gain: bfloat16 [1024], P('shard'), may hold values from 0.5 to 1.5
- qkv_weight: bfloat16 [1024, 3072], P('shard'), may hold values from -0.1875 to 0.1875
- out_weight: bfloat16 [1024, 1024], P('shard'), may hold values from -1 to 1
- norm2_gain: bfloat16 [1024], P('shard'), may hold values from 0.5 to 1.5
- mix_weight: bfloat16 [1024, 2], P('shard'), may hold values from -0.1875 to 0.1875
- dense_in: bfloat16 [1024, 4096], P('shard'), may hold values from -0.1875 to 0.1875
- dense_out: bfloat16 [4096, 1024], P('shard'), may hold values from -0.1875 to 0.1875
- expert_in: bfloat16 [8, 1024, 4096], P('expert', None, 'shard'), may hold values from -0.1875 to 0.1875
- expert_out: bfloat16 [8, 4096, 1024], P('expert', 'shard'), may hold values from -0.1875 to 0.1875
Outputs:
- output: bfloat16 [2, 4, 1024, 1024], P(None, 'expert', 'shard')
- input_grad: bfloat16 [2, 4, 1024, 1024], P(None, 'expert', 'shard')
- norm1_gain_grad: float32 [1024], P('shard')
- qkv_grad: float32 [1024, 3072], P('shard')
- out_grad: float32 [1024, 1024], P('shard')
- norm2_gain_grad: float32 [1024], P('shard')
- mix_grad: float32 [1024, 2], P('shard')
- dense_in_grad: float32 [1024, 4096], P('shard')
- dense_out_grad: float32 [4096, 1024], P('shard')
- expert_in_grad: float32 [8, 1024, 4096], P('expert', None, 'shard')
- expert_out_grad: float32 [8, 4096, 1024], P('expert', 'shard')
Inputs may be any that keep to these rules, and one draw needn't show every extreme that they name: `segments`: within every sequence the numbers never fall; each document has at most 512 positions. `routes`: in each aligned block of 128 positions of a sequence and micro-batch, no expert is named more than 32 times, and in every draw some expert is named exactly 32 times in some block.
All inputs are finite; a program needn't handle non-finite values.
Results may differ from a plain program's by a relative error of at most 0.02.
Values may be sent and summed in bfloat16 or wider, within the bound.
No kernel may reach another device: no remote copies, remote signals or barrier semaphores. Data moves between devices by JAX's collectives and lax.ppermute only.
A program may use at most 176 MiB of HBM per device.

v0:
```python
import jax
import jax.numpy as jnp
from jax import lax
from jax.sharding import PartitionSpec as P

HEADS = 16
HEAD_DIM = 64


def layer_norm(values, gain):
    center = jnp.mean(values, axis=-1, keepdims=True)
    shifted = values - center
    spread = jnp.mean(shifted * shifted, axis=-1, keepdims=True)
    return shifted * lax.rsqrt(spread + 1e-05) * gain


def activate(values):
    return jax.nn.gelu(values, approximate=True)


def fetch_weights(gain_one, w_qkv, w_attn, gain_two, w_mix, w_in, w_down):
    return (
        lax.all_gather(gain_one, "shard", axis=0, tiled=True),
        lax.all_gather(w_qkv, "shard", axis=0, tiled=True),
        lax.all_gather(w_attn, "shard", axis=0, tiled=True),
        lax.all_gather(gain_two, "shard", axis=0, tiled=True),
        lax.all_gather(w_mix, "shard", axis=0, tiled=True),
        lax.all_gather(w_in, "shard", axis=0, tiled=True),
        lax.all_gather(w_down, "shard", axis=0, tiled=True),
    )


def reduce_grads(grad_one, grad_qkv, grad_attn, grad_two, grad_mix, grad_in, grad_down):
    return (
        lax.psum_scatter(
            grad_one.astype(jnp.bfloat16), "shard", scatter_dimension=0, tiled=True
        ).astype(jnp.float32),
        lax.psum_scatter(
            grad_qkv.astype(jnp.bfloat16), "shard", scatter_dimension=0, tiled=True
        ).astype(jnp.float32),
        lax.psum_scatter(
            grad_attn.astype(jnp.bfloat16), "shard", scatter_dimension=0, tiled=True
        ).astype(jnp.float32),
        lax.psum_scatter(
            grad_two.astype(jnp.bfloat16), "shard", scatter_dimension=0, tiled=True
        ).astype(jnp.float32),
        lax.psum_scatter(
            grad_mix.astype(jnp.bfloat16), "shard", scatter_dimension=0, tiled=True
        ).astype(jnp.float32),
        lax.psum_scatter(
            grad_in.astype(jnp.bfloat16), "shard", scatter_dimension=0, tiled=True
        ).astype(jnp.float32),
        lax.psum_scatter(
            grad_down.astype(jnp.bfloat16), "shard", scatter_dimension=0, tiled=True
        ).astype(jnp.float32),
    )


def add_trees(first, second):
    if first is None:
        return second
    return jax.tree.map(jnp.add, first, second)


def per_device(
    tokens,
    segments,
    routes,
    cotangent,
    norm1_gain,
    qkv_weight,
    out_weight,
    norm2_gain,
    mix_weight,
    dense_in,
    dense_out,
    expert_in,
    expert_out,
):
    highest = lax.Precision.HIGHEST
    micro = tokens.shape[0]
    rows = tokens.shape[2]
    width = tokens.shape[3]
    seq_len = segments.shape[2]
    n_expert = lax.axis_size("expert")
    local_experts = expert_in.shape[0]
    experts = local_experts * n_expert
    capacity = max(2, 2 * rows // experts)
    start = lax.axis_index("shard") * rows
    query_pos = start + jnp.arange(rows, dtype=jnp.int32)
    key_pos = jnp.arange(seq_len, dtype=jnp.int32)
    slot_ids = jnp.arange(experts * capacity, dtype=jnp.int32)
    expert_ids = jnp.arange(experts, dtype=jnp.int32)
    scale = HEAD_DIM ** (-0.5)
    grads_acc = None
    expert_in_acc = jnp.zeros(expert_in.shape, jnp.float32)
    expert_out_acc = jnp.zeros(expert_out.shape, jnp.float32)
    outputs = []
    input_grads = []
    for index in range(micro):
        weights = fetch_weights(
            norm1_gain, qkv_weight, out_weight, norm2_gain, mix_weight, dense_in, dense_out
        )
        gain_one, qkv_full, attn_full, gain_two, mix_full, in_full, down_full = weights
        inputs = tokens[index, 0].astype(jnp.float32)
        seg_all = segments[index, 0]
        seg_query = lax.dynamic_slice_in_dim(seg_all, start, rows)
        route = routes[index, 0, :, 0]
        allowed = (key_pos[None, :] <= query_pos[:, None]) & (
            seg_query[:, None] == seg_all[None, :]
        )
        normed_f, norm_one_back = jax.vjp(layer_norm, inputs, gain_one.astype(jnp.float32))
        normed_one = normed_f.astype(jnp.bfloat16)
        qkv = jnp.dot(normed_one, qkv_full, preferred_element_type=jnp.float32).astype(jnp.bfloat16)
        queries = qkv[:, :width].reshape(rows, HEADS, HEAD_DIM)
        keys_own = qkv[:, width : 2 * width].reshape(rows, HEADS, HEAD_DIM)
        values_own = qkv[:, 2 * width :].reshape(rows, HEADS, HEAD_DIM)
        keys_all, values_all = (
            lax.all_gather(keys_own, "shard", axis=0, tiled=True),
            lax.all_gather(values_own, "shard", axis=0, tiled=True),
        )
        scores = (
            jnp.einsum("qhd,khd->hqk", queries, keys_all, preferred_element_type=jnp.float32)
            * scale
        )
        masked = jnp.where(allowed[None], scores, -1e30)
        row_max = jnp.max(masked, axis=-1, keepdims=True)
        weights_exp = jnp.where(allowed[None], jnp.exp(scores - row_max), 0.0)
        row_total = jnp.sum(weights_exp, axis=-1, keepdims=True)
        probs = weights_exp / row_total
        heads_out = (
            jnp.einsum(
                "hqk,khd->qhd",
                probs.astype(jnp.bfloat16),
                values_all,
                preferred_element_type=jnp.float32,
            )
            .astype(jnp.bfloat16)
            .reshape(rows, width)
        )
        mid = inputs + jnp.dot(heads_out, attn_full, preferred_element_type=jnp.float32)
        normed_t, norm_two_back = jax.vjp(layer_norm, mid, gain_two.astype(jnp.float32))
        normed_two = normed_t.astype(jnp.bfloat16)
        dense_up = jnp.dot(normed_two, in_full, preferred_element_type=jnp.float32)
        dense_act_f, dense_act_back = jax.vjp(activate, dense_up)
        dense_act = dense_act_f.astype(jnp.bfloat16)
        dense_branch = jnp.dot(dense_act, down_full, preferred_element_type=jnp.float32)
        logits = jnp.dot(normed_two, mix_full, preferred_element_type=jnp.float32)
        mixing, mixing_back = jax.vjp(lambda values: jax.nn.softmax(values, axis=-1), logits)
        onehot = (route[:, None] == expert_ids[None, :]).astype(jnp.int32)
        rank = jnp.sum((jnp.cumsum(onehot, axis=0) - onehot) * onehot, axis=1)
        slot = route * capacity + rank
        placing = (slot[None, :] == slot_ids[:, None]).astype(jnp.bfloat16)
        sent = jnp.dot(placing, normed_two, preferred_element_type=jnp.float32).astype(jnp.bfloat16)
        sent = sent.reshape(n_expert, local_experts, capacity, width)
        arrived = lax.all_to_all(sent, "expert", split_axis=0, concat_axis=0, tiled=True)
        expert_rows = lax.all_gather(arrived, "shard", axis=0, tiled=True)
        expert_up = jnp.einsum(
            "sjcd,jdf->sjcf", expert_rows, expert_in, preferred_element_type=jnp.float32
        )
        expert_act_f, expert_act_back = jax.vjp(activate, expert_up)
        expert_act = expert_act_f.astype(jnp.bfloat16)
        partial_out = jnp.einsum(
            "sjcf,jfd->sjcd", expert_act, expert_out, preferred_element_type=jnp.float32
        )
        summed_out = lax.psum_scatter(partial_out, "shard", scatter_dimension=0, tiled=True).astype(
            jnp.bfloat16
        )
        returned = lax.all_to_all(
            summed_out, "expert", split_axis=0, concat_axis=0, tiled=True
        ).reshape(experts * capacity, width)
        expert_branch = jnp.einsum(
            "st,sd->td", placing, returned, preferred_element_type=jnp.float32
        )
        mixed = mid + mixing[:, 0:1] * dense_branch + mixing[:, 1:2] * expert_branch
        outputs.append(mixed.astype(jnp.bfloat16))
        grad_y = cotangent[index, 0].astype(jnp.float32)
        grad_mix_c = jnp.stack(
            [jnp.sum(grad_y * dense_branch, axis=-1), jnp.sum(grad_y * expert_branch, axis=-1)],
            axis=-1,
        )
        grad_logits = mixing_back(grad_mix_c)[0]
        grad_dense_branch = (mixing[:, 0:1] * grad_y).astype(jnp.bfloat16)
        grad_expert_branch = (mixing[:, 1:2] * grad_y).astype(jnp.bfloat16)
        grad_down = jnp.einsum(
            "tf,td->fd", dense_act, grad_dense_branch, preferred_element_type=jnp.float32
        )
        grad_dense_act = jnp.einsum(
            "td,fd->tf", grad_dense_branch, down_full, preferred_element_type=jnp.float32
        )
        grad_dense_up = dense_act_back(grad_dense_act)[0].astype(jnp.bfloat16)
        grad_in = jnp.einsum(
            "td,tf->df", normed_two, grad_dense_up, preferred_element_type=jnp.float32
        )
        grad_normed_two = jnp.einsum(
            "tf,df->td", grad_dense_up, in_full, preferred_element_type=jnp.float32
        )
        normed_wide = normed_two.astype(jnp.float32)
        grad_mix = jnp.einsum("td,tc->dc", normed_wide, grad_logits, precision=highest)
        grad_normed_two = grad_normed_two + jnp.einsum(
            "tc,dc->td", grad_logits, mix_full.astype(jnp.float32), precision=highest
        )
        grad_sent = jnp.dot(placing, grad_expert_branch, preferred_element_type=jnp.float32).astype(
            jnp.bfloat16
        )
        grad_sent = grad_sent.reshape(n_expert, local_experts, capacity, width)
        grad_arrived = lax.all_to_all(grad_sent, "expert", split_axis=0, concat_axis=0, tiled=True)
        grad_expert_rows = lax.all_gather(grad_arrived, "shard", axis=0, tiled=True)
        grad_expert_act = jnp.einsum(
            "sjcd,jfd->sjcf", grad_expert_rows, expert_out, preferred_element_type=jnp.float32
        )
        grad_expert_up = expert_act_back(grad_expert_act)[0].astype(jnp.bfloat16)
        expert_out_acc = expert_out_acc + jnp.einsum(
            "sjcf,sjcd->jfd", expert_act, grad_expert_rows, preferred_element_type=jnp.float32
        )
        expert_in_acc = expert_in_acc + jnp.einsum(
            "sjcd,sjcf->jdf", expert_rows, grad_expert_up, preferred_element_type=jnp.float32
        )
        grad_partial = jnp.einsum(
            "sjcf,jdf->sjcd", grad_expert_up, expert_in, preferred_element_type=jnp.float32
        )
        grad_summed = lax.psum_scatter(
            grad_partial, "shard", scatter_dimension=0, tiled=True
        ).astype(jnp.bfloat16)
        grad_returned = lax.all_to_all(
            grad_summed, "expert", split_axis=0, concat_axis=0, tiled=True
        ).reshape(experts * capacity, width)
        grad_normed_two = grad_normed_two + jnp.einsum(
            "st,sd->td", placing, grad_returned, preferred_element_type=jnp.float32
        )
        grad_mid_norm, grad_two = norm_two_back(grad_normed_two)
        grad_mid = grad_y + grad_mid_norm
        grad_attn_out = grad_mid.astype(jnp.bfloat16)
        grad_attn = jnp.einsum(
            "td,te->de", heads_out, grad_attn_out, preferred_element_type=jnp.float32
        )
        grad_heads = (
            jnp.einsum("te,de->td", grad_attn_out, attn_full, preferred_element_type=jnp.float32)
            .astype(jnp.bfloat16)
            .reshape(rows, HEADS, HEAD_DIM)
        )
        scores_again = (
            jnp.einsum("qhd,khd->hqk", queries, keys_all, preferred_element_type=jnp.float32)
            * scale
        )
        probs_again = jnp.where(allowed[None], jnp.exp(scores_again - row_max), 0.0) / row_total
        grad_probs = jnp.einsum(
            "qhd,khd->hqk", grad_heads, values_all, preferred_element_type=jnp.float32
        )
        delta = jnp.sum(grad_probs * probs_again, axis=-1, keepdims=True)
        grad_scores = (probs_again * (grad_probs - delta)).astype(jnp.bfloat16)
        grad_queries = (
            jnp.einsum("hqk,khd->qhd", grad_scores, keys_all, preferred_element_type=jnp.float32)
            * scale
        )
        grad_keys_part = (
            jnp.einsum("hqk,qhd->khd", grad_scores, queries, preferred_element_type=jnp.float32)
            * scale
        )
        grad_values_part = jnp.einsum(
            "hqk,qhd->khd",
            probs_again.astype(jnp.bfloat16),
            grad_heads,
            preferred_element_type=jnp.float32,
        )
        grad_keys, grad_values = (
            lax.psum_scatter(grad_keys_part, "shard", scatter_dimension=0, tiled=True),
            lax.psum_scatter(grad_values_part, "shard", scatter_dimension=0, tiled=True),
        )
        grad_qkv_rows = jnp.concatenate(
            [
                grad_queries.reshape(rows, width),
                grad_keys.reshape(rows, width),
                grad_values.reshape(rows, width),
            ],
            axis=1,
        ).astype(jnp.bfloat16)
        grad_qkv = jnp.einsum(
            "td,te->de", normed_one, grad_qkv_rows, preferred_element_type=jnp.float32
        )
        grad_normed_one = jnp.einsum(
            "te,de->td", grad_qkv_rows, qkv_full, preferred_element_type=jnp.float32
        )
        grad_input_norm, grad_one = norm_one_back(grad_normed_one)
        input_grads.append((grad_mid + grad_input_norm).astype(jnp.bfloat16))
        shares = reduce_grads(grad_one, grad_qkv, grad_attn, grad_two, grad_mix, grad_in, grad_down)
        grads_acc = add_trees(grads_acc, shares)
    totals = (
        lax.psum(grads_acc[0].astype(jnp.bfloat16), "expert").astype(jnp.float32),
        lax.psum(grads_acc[1].astype(jnp.bfloat16), "expert").astype(jnp.float32),
        lax.psum(grads_acc[2].astype(jnp.bfloat16), "expert").astype(jnp.float32),
        lax.psum(grads_acc[3].astype(jnp.bfloat16), "expert").astype(jnp.float32),
        lax.psum(grads_acc[4].astype(jnp.bfloat16), "expert").astype(jnp.float32),
        lax.psum(grads_acc[5].astype(jnp.bfloat16), "expert").astype(jnp.float32),
        lax.psum(grads_acc[6].astype(jnp.bfloat16), "expert").astype(jnp.float32),
    )
    output = jnp.stack(outputs)[:, None]
    input_grad = jnp.stack(input_grads)[:, None]
    return (
        output,
        input_grad,
        totals[0],
        totals[1],
        totals[2],
        totals[3],
        totals[4],
        totals[5],
        totals[6],
        expert_in_acc,
        expert_out_acc,
    )


def solution(mesh):
    return jax.shard_map(
        per_device,
        mesh=mesh,
        in_specs=(
            P(None, "expert", "shard", None),
            P(None, "expert", None),
            P(None, "expert", "shard", None),
            P(None, "expert", "shard", None),
            P("shard"),
            P("shard", None),
            P("shard", None),
            P("shard"),
            P("shard", None),
            P("shard", None),
            P("shard", None),
            P("expert", None, "shard"),
            P("expert", "shard", None),
        ),
        out_specs=(
            P(None, "expert", "shard", None),
            P(None, "expert", "shard", None),
            P("shard"),
            P("shard", None),
            P("shard", None),
            P("shard"),
            P("shard", None),
            P("shard", None),
            P("shard", None),
            P("expert", None, "shard"),
            P("expert", "shard", None),
        ),
        check_vma=False,
    )
```

profile of v0, /device:TPU:0, one launch (start us, length us, event | category | flops | bytes accessed | tf_op | source)
XLA Modules:
  0.0 2181.3 jit_solution(6817090226531772523)
XLA Ops:
  8.0 10.4 all-gather
  21.5 36.5 %all-gather.15.cloned.1.call-done = bf16[1024,3072]{1,0:T(8,128)(2,1)} async-done(((bf16[128,3072]{1,0:T(8,128)(2,1)}), bf16[1024,3072]{1,0:T(8,128)(2,1)}) %all-gather.15.cloned.1.call-update) | async-done | bytes 6291472 | tf_op jit(solution)/shard_map/all_gather | solution.py:24
  75.7 9.3 all-gather.1
  87.0 5.8 all-gather.19.cloned.1.call-done
  92.9 9.5 fusion.190
  102.4 21.1 all-gather.17.cloned.1.call-done
  123.5 6.4 fusion.72
  129.9 23.2 %all-gather.21.cloned.1.call-done = bf16[1024,1024]{1,0:T(8,128)(2,1)} async-done(((bf16[128,1024]{1,0:T(8,128)(2,1)}), bf16[1024,1024]{1,0:T(8,128)(2,1)}) %all-gather.21.cloned.1.call-update) | async-done | bytes 2097168 | tf_op jit(solution)/shard_map/all_gather | solution.py:25
  156.0 27.5 %all-gather.31.cloned.1.call-done = bf16[1024,16,64]{0,2,1:T(8,128)(2,1)} async-done(((bf16[128,16,64]{0,2,1:T(8,128)(2,1)}), bf16[1024,16,64]{0,2,1:T(8,128)(2,1)}) %all-gather.31.cloned.1.call-update) | async-done | bytes 2097168 | tf_op jit(solution)/shard_map/all_gather | solution.py:119
  183.5 10.0 fusion.192
  193.5 20.4 all-gather.29.cloned.1.call-done
  213.9 5.8 fusion.75
  221.8 19.3 all_to_all.40
  242.3 16.7 all_to_all.41
  259.9 9.0 all_gather.58
  270.7 17.7 all_to_all.42
  296.8 13.0 all-to-all-done.4
  311.8 6.2 fusion.196
  320.6 5.6 all-gather.25.cloned.1.call-done
  326.3 7.8 fusion.44
  334.1 8.0 fusion.198
  346.6 18.8 all-gather.33.cloned.1.call-done
  372.6 6.3 convolution_bitcast_fusion.2
  378.8 25.5 %all-gather.27.cloned.1.call-done = bf16[32,2,32,1024]{3,2,0,1:T(8,128)(2,1)} async-done(((bf16[4,2,32,1024]{3,2,0,1:T(8,128)(2,1)}), bf16[32,2,32,1024]{3,2,0,1:T(8,128)(2,1)}) %all-gather.27.cloned.1.call-update) | async-done | bytes 4194320 | tf_op jit(solution)/shard_map/all_gather | solution.py:157
  411.5 5.8 convolution_bitcast_fusion.3
  417.4 26.0 %all-gather.37.cloned.1.call-done = bf16[32,2,32,1024]{3,2,0,1:T(8,128)(2,1)} async-done(((bf16[4,2,32,1024]{3,2,0,1:T(8,128)(2,1)}), bf16[32,2,32,1024]{3,2,0,1:T(8,128)(2,1)}) %all-gather.37.cloned.1.call-update) | async-done | bytes 4194320 | tf_op jit(solution)/shard_map/all_gather | solution.py:208
  443.4 7.9 fusion.23
  452.6 5.6 convolution_bitcast_fusion
  458.2 23.5 %all-gather.35.cloned.1.call-done = bf16[32,2,32,1024]{3,2,0,1:T(8,128)(2,1)} async-done(((bf16[4,2,32,1024]{3,2,0,1:T(8,128)(2,1)}), bf16[32,2,32,1024]{3,2,0,1:T(8,128)(2,1)}) %all-gather.35.cloned.1.call-update) | async-done | bytes 4194320 | tf_op jit(solution)/shard_map/all_gather | solution.py:208
  481.8 7.9 fusion.16
  491.0 5.6 convolution_bitcast_fusion.1
  496.6 650.2 %all-reduce.16 = (bf16[32,2,32,1024]{3,2,0,1:T(8,128)(2,1)}, bf16[32,2,32,1024]{3,2,0,1:T(8,128)(2,1)}, bf16[32,2,32,1024]{3,2,0,1:T(8,128)(2,1)}, bf16[32,2,32,1024]{3,2,0,1:T(8,128)(2,1)}) all-reduce(f32[32,2,32,1024]{3,2,0,1:T(8,128)} %convolution_bitcast_fusion.2, ...), channel_id=3, replica_groups=mesh['shard'=8,'expert'=4] {'shard'}, use_global_device_ids=true, to_apply=%region_21.22.clone | all-reduce | flops 8388608 | bytes 50331648
  1153.3 7.5 fusion.199
  1172.5 5.7 fusion.178
  1180.2 6.3 all-to-all-done.1
  1190.0 6.4 fusion.179
  1198.4 5.6 all-to-all-done.7
  1212.5 9.8 all-to-all-done.5
  1229.2 6.3 convolution_bitcast_fusion.4
  1235.6 5.7 multiply_reduce_fusion
  1252.4 6.2 convolution_bitcast_fusion.5
  1258.6 5.7 multiply_reduce_fusion.1
  1279.0 5.7 convolution_convert_fusion
  1286.3 5.7 convolution_convert_fusion.1
  1293.4 6.1 convolution_convert_fusion.2
  1300.9 5.6 convolution_convert_fusion.3
  1312.3 27.8 %reduce-scatter.35.cloned.1.call-done = f32[128,16,64]{0,2,1:T(8,128)} async-done(((f32[1024,16,64]{0,2,1:T(8,128)}), f32[128,16,64]{0,2,1:T(8,128)}) %reduce-scatter.35.cloned.1.call-update) | async-done | bytes 524304 | tf_op jit(solution)/shard_map/reduce_scatter | solution.py:267
  1350.2 44.1 %reduce-scatter.33.cloned.1.call-done = f32[128,16,64]{0,2,1:T(8,128)} async-done(((f32[1024,16,64]{0,2,1:T(8,128)}), f32[128,16,64]{0,2,1:T(8,128)}) %reduce-scatter.33.cloned.1.call-update) | async-done | bytes 524304 | tf_op jit(solution)/shard_map/reduce_scatter | solution.py:268
  1395.4 53.2 %reduce-scatter.31.cloned.1.call-done = f32[128,16,64]{0,2,1:T(8,128)} async-done(((f32[1024,16,64]{0,2,1:T(8,128)}), f32[128,16,64]{0,2,1:T(8,128)}) %reduce-scatter.31.cloned.1.call-update) | async-done | bytes 524304 | tf_op jit(solution)/shard_map/reduce_scatter | solution.py:267
  1455.3 7.5 fusion.200
  1473.9 19.0 reduce-scatter.45.cloned.1.call-done
  1492.9 44.3 %reduce-scatter.43.cloned.1.call-done = bf16[128,1024]{1,0:T(8,128)(2,1)} async-done(((bf16[1024,1024]{1,0:T(8,128)(2,1)}), bf16[128,1024]{1,0:T(8,128)(2,1)}) %reduce-scatter.43.cloned.1.call-update) | async-done | bytes 262160 | tf_op jit(solution)/shard_map/reduce_scatter | solution.py:41
  1539.0 73.2 %reduce-scatter.53.cloned.1.call-done = bf16[512,1024]{1,0:T(8,128)(2,1)} async-done(((bf16[4096,1024]{1,0:T(8,128)(2,1)}), bf16[512,1024]{1,0:T(8,128)(2,1)}) %reduce-scatter.53.cloned.1.call-update) | async-done | bytes 1048592 | tf_op jit(solution)/shard_map/reduce_scatter | solution.py:53
  1612.2 74.9 %reduce-scatter.51.cloned.1.call-done = bf16[512,1024]{1,0:T(8,128)(2,1)} async-done(((bf16[4096,1024]{1,0:T(8,128)(2,1)}), bf16[512,1024]{1,0:T(8,128)(2,1)}) %reduce-scatter.51.cloned.1.call-update) | async-done | bytes 1048592 | tf_op jit(solution)/shard_map/reduce_scatter | solution.py:53
  1690.0 72.1 %reduce-scatter.49.cloned.1.call-done = bf16[128,4096]{1,0:T(8,128)(2,1)} async-done(((bf16[1024,4096]{1,0:T(8,128)(2,1)}), bf16[128,4096]{1,0:T(8,128)(2,1)}) %reduce-scatter.49.cloned.1.call-update) | async-done | bytes 1048592 | tf_op jit(solution)/shard_map/reduce_scatter | solution.py:50
  1762.1 75.0 %reduce-scatter.47.cloned.1.call-done = bf16[128,4096]{1,0:T(8,128)(2,1)} async-done(((bf16[1024,4096]{1,0:T(8,128)(2,1)}), bf16[128,4096]{1,0:T(8,128)(2,1)}) %reduce-scatter.47.cloned.1.call-update) | async-done | bytes 1048592 | tf_op jit(solution)/shard_map/reduce_scatter | solution.py:50
  1839.8 62.4 %reduce-scatter.41.cloned.1.call-done = bf16[128,3072]{1,0:T(8,128)(2,1)} async-done(((bf16[1024,3072]{1,0:T(8,128)(2,1)}), bf16[128,3072]{1,0:T(8,128)(2,1)}) %reduce-scatter.41.cloned.1.call-update) | async-done | bytes 786448 | tf_op jit(solution)/shard_map/reduce_scatter | solution.py:38
  1902.2 65.0 %reduce-scatter.39.cloned.1.call-done = bf16[128,3072]{1,0:T(8,128)(2,1)} async-done(((bf16[1024,3072]{1,0:T(8,128)(2,1)}), bf16[128,3072]{1,0:T(8,128)(2,1)}) %reduce-scatter.39.cloned.1.call-update) | async-done | bytes 786448 | tf_op jit(solution)/shard_map/reduce_scatter | solution.py:38
  1969.7 8.5 bitcast_add_fusion.1
  1979.0 24.9 %reduce-scatter.57.cloned.1.call-done = bf16[128,2]{1,0:T(8,128)(2,1)} async-done(((bf16[1024,2]{1,0:T(8,128)(2,1)}), bf16[128,2]{1,0:T(8,128)(2,1)}) %reduce-scatter.57.cloned.1.call-update) | async-done | bytes 528
  2004.8 35.8 %reduce-scatter.55.cloned.1.call-done = bf16[128,2]{1,0:T(8,128)(2,1)} async-done(((bf16[1024,2]{1,0:T(8,128)(2,1)}), bf16[128,2]{1,0:T(8,128)(2,1)}) %reduce-scatter.55.cloned.1.call-update) | async-done | bytes 528
  2052.4 13.2 all-reduce.9
  2065.8 12.2 all-reduce.10
  2080.9 84.5 %all-reduce.15.cloned.1.call-done = (bf16[128,3072]{1,0:T(8,128)(2,1)}, bf16[128,1024]{1,0:T(8,128)(2,1)}, bf16[128,4096]{1,0:T(8,128)(2,1)}, bf16[512,1024]{1,0:T(8,128)(2,1)}) async-done(((bf16[128,3072]{1,0:T(8,128)(2,1)}, bf16[128,1024]{1,0:T(8,128)(2,1)}, bf16[128,4096]{1,0:T(8,128)(2,1)}, bf16[512,1024]{1,0:T(8,128)(2,1)}), (bf16[128,3072]{1,0:T(8,128)(2,1)}, bf16[128,1024]{1,0:T(8,128)(2,1)}, ...) | async-done | bytes 3145744 | tf_op jit(solution)/shard_map/psum | solution.py:290
  (415 shorter events, 205.7 us)
Async XLA Ops:
  7.2 365.4 %copy-start = (bf16[2,512,1024]{2,1,0:T(8,128)(2,1)S(1)}, bf16[2,512,1024]{2,1,0:T(8,128)(2,1)}, u32[]{:S(2)}) copy-start(bf16[2,512,1024]{2,1,0:T(8,128)(2,1)} %param.25) | copy-start | bytes 6291460
  7.2 50.8 %all-gather.15.cloned.1.call-start = ((), (), s32[]{:S(2)}) async-start(), calls=%async_computation.22 | async-start | bytes 7077888 | tf_op jit(solution)/shard_map/all_gather | solution.py:24
  7.9 85.0 %all-gather.19.cloned.1.call-start = ((), (), s32[]{:S(2)}) async-start(), calls=%async_computation.24 | async-start | bytes 2359296 | tf_op jit(solution)/shard_map/all_gather | solution.py:119
  18.4 47.8 %copy-start.40 = (f32[8,1,128]{2,1,0:T(1,128)}, f32[8,1,128]{2,1,0:T(1,128)S(1)}, u32[]{:S(2)}) copy-start(f32[8,1,128]{2,1,0:T(1,128)S(1)} %convert_element_type.398) | copy-start | bytes 12292
  19.6 42.4 %copy-start.55 = (f32[128]{0:T(128)}, f32[128]{0:T(128)S(1)}, u32[]{:S(2)}) copy-start(f32[128]{0:T(128)S(1)} %broadcast_multiply_fusion.3) | copy-start | bytes 1540
  19.6 46.6 %copy-start.57 = (f32[128]{0:T(128)}, f32[128]{0:T(128)S(1)}, u32[]{:S(2)}) copy-start(f32[128]{0:T(128)S(1)} %broadcast_multiply_fusion.1) | copy-start | bytes 1540
  21.0 45.1 %copy-start.96 = (f32[128]{0:T(128)}, f32[128]{0:T(128)S(1)}, u32[]{:S(2)}) copy-start(f32[128]{0:T(128)S(1)} %get-tuple-element.61) | copy-start | bytes 1540
  21.5 40.5 %copy-start.61 = (f32[128]{0:T(128)}, f32[128]{0:T(128)S(1)}, u32[]{:S(2)}) copy-start(f32[128]{0:T(128)S(1)} %fusion.158) | copy-start | bytes 1540
  64.6 58.8 %all-gather.17.cloned.1.call-start = ((), (), s32[]{:S(2)}) async-start(), calls=%async_computation.23 | async-start | bytes 2359296 | tf_op jit(solution)/shard_map/all_gather | solution.py:120
  65.5 87.5 %all-gather.21.cloned.1.call-start = ((), (), s32[]{:S(2)}) async-start(), calls=%async_computation.25 | async-start | bytes 2359296 | tf_op jit(solution)/shard_map/all_gather | solution.py:25
  66.1 117.3 %all-gather.31.cloned.1.call-start = ((), (), s32[]{:S(2)}) async-start(), calls=%async_computation.30 | async-start | bytes 2359296 | tf_op jit(solution)/shard_map/all_gather | solution.py:119
  73.2 140.7 %all-gather.29.cloned.1.call-start = ((), (), s32[]{:S(2)}) async-start(), calls=%async_computation.29 | async-start | bytes 2359296 | tf_op jit(solution)/shard_map/all_gather | solution.py:120
  74.1 237.6 %all-gather.23.cloned.1.call-start = ((), (), s32[]{:S(2)}) async-start(), calls=%async_computation.26 | async-start | bytes 9437184 | tf_op jit(solution)/shard_map/all_gather | solution.py:28
  74.9 251.4 %all-gather.25.cloned.1.call-start = ((), (), s32[]{:S(2)}) async-start(), calls=%async_computation.27 | async-start | bytes 9437184 | tf_op jit(solution)/shard_map/all_gather | solution.py:29
  75.6 289.7 %all-gather.33.cloned.1.call-start = ((), (), s32[]{:S(2)}) async-start(), calls=%async_computation.31 | async-start | bytes 4718592 | tf_op jit(solution)/shard_map/all_gather | solution.py:157
  102.4 27.4 %copy-start.73 = (f32[16,128]{1,0:T(8,128)}, f32[16,128]{1,0:T(8,128)S(1)}, u32[]{:S(2)}) copy-start(f32[16,128]{1,0:T(8,128)S(1)} %get-tuple-element.113) | copy-start | bytes 24580
  219.7 21.4 copy-start.50
  221.1 38.8 %copy-start.95 = (bf16[128,2]{0,1:T(2,128)(2,1)S(1)}, bf16[128,2]{0,1:T(2,128)(2,1)}, u32[]{:S(2)}) copy-start(bf16[128,2]{0,1:T(2,128)(2,1)} %param.21) | copy-start | bytes 1540
  221.5 90.3 %copy-start.15 = (bf16[128,1024]{1,0:T(8,128)(2,1)}, bf16[128,1024]{1,0:T(8,128)(2,1)S(1)}, u32[]{:S(2)}) copy-start(bf16[128,1024]{1,0:T(8,128)(2,1)S(1)} %get-tuple-element.101) | copy-start | bytes 786436
  221.5 96.5 %copy-start.17 = (bf16[128,1024]{1,0:T(8,128)(2,1)}, bf16[128,1024]{1,0:T(8,128)(2,1)S(1)}, u32[]{:S(2)}) copy-start(bf16[128,1024]{1,0:T(8,128)(2,1)S(1)} %get-tuple-element.102) | copy-start | bytes 786436
  242.0 162.3 %all-gather.27.cloned.1.call-start = ((), (), s32[]{:S(2)}) async-start(), calls=%async_computation.28 | async-start | bytes 4718592 | tf_op jit(solution)/shard_map/all_gather | solution.py:157
  242.3 53.3 %copy-start.104 = (u32[32]{0:T(128)S(1)}, u32[32]{0:T(128)}, u32[]{:S(2)}) copy-start(u32[32]{0:T(128)} %constant.84) | copy-start | bytes 388
  259.9 183.6 %all-gather.37.cloned.1.call-start = ((), (), s32[]{:S(2)}) async-start(), calls=%async_computation.35 | async-start | bytes 4718592 | tf_op jit(solution)/shard_map/all_gather | solution.py:208
  269.0 955.0 %copy-start.51 = (f32[128,2]{0,1:T(2,128)}, f32[128,2]{0,1:T(2,128)S(1)}, u32[]{:S(2)}) copy-start(f32[128,2]{0,1:T(2,128)S(1)} %get-tuple-element.124) | copy-start | bytes 3076
  269.1 955.0 %copy-start.65 = (f32[128]{0:T(128)}, f32[128]{0:T(128)S(1)}, u32[]{:S(2)}) copy-start(f32[128]{0:T(128)S(1)} %get-tuple-element.123) | copy-start | bytes 1540
  269.2 954.3 %copy-start.53 = (f32[128,2]{0,1:T(2,128)}, f32[128,2]{0,1:T(2,128)S(1)}, u32[]{:S(2)}) copy-start(f32[128,2]{0,1:T(2,128)S(1)} %get-tuple-element.122) | copy-start | bytes 3076
  269.3 954.3 %copy-start.59 = (f32[128]{0:T(128)}, f32[128]{0:T(128)S(1)}, u32[]{:S(2)}) copy-start(f32[128]{0:T(128)S(1)} %get-tuple-element.121) | copy-start | bytes 1540
  269.3 954.3 %copy-start.71 = (f32[128]{0:T(128)}, f32[128]{0:T(128)S(1)}, u32[]{:S(2)}) copy-start(f32[128]{0:T(128)S(1)} %get-tuple-element.132) | copy-start | bytes 1540
  269.3 954.8 %copy-start.82 = (f32[128]{0:T(128)}, f32[128]{0:T(128)S(1)}, u32[]{:S(2)}) copy-start(f32[128]{0:T(128)S(1)} %get-tuple-element.131) | copy-start | bytes 1540
  291.4 18.4 all-to-all-start.4
  295.5 186.3 %all-gather.35.cloned.1.call-start = ((), (), s32[]{:S(2)}) async-start(), calls=%async_computation.32 | async-start | bytes 4718592 | tf_op jit(solution)/shard_map/all_gather | solution.py:208
  326.3 15.8 copy-start.101
  1148.7 19.4 all-to-all-start.3
  1153.3 19.2 copy-start.11
  1168.8 17.7 all-to-all-start.1
  1186.5 17.5 all-to-all-start.7
  1198.4 25.2 %copy-start.32 = (f32[128,1024]{1,0:T(8,128)S(1)}, f32[128,1024]{1,0:T(8,128)}, u32[]{:S(2)}) copy-start(f32[128,1024]{1,0:T(8,128)} %fusion.199) | copy-start | bytes 1572868
  1204.0 18.2 all-to-all-start.5
  1208.2 103.0 %reduce-scatter.37.cloned.1.call-start = ((), (), s32[]{:S(2)}) async-start(), calls=%async_computation.37 | async-start | bytes 4718592 | tf_op jit(solution)/shard_map/reduce_scatter | solution.py:268
  1235.5 104.5 %reduce-scatter.35.cloned.1.call-start = ((), (), s32[]{:S(2)}) async-start(), calls=%async_computation.36 | async-start | bytes 4718592 | tf_op jit(solution)/shard_map/reduce_scatter | solution.py:267
  1251.1 143.2 %reduce-scatter.33.cloned.1.call-start = ((), (), s32[]{:S(2)}) async-start(), calls=%async_computation.34 | async-start | bytes 4718592 | tf_op jit(solution)/shard_map/reduce_scatter | solution.py:268
  1258.6 190.1 %reduce-scatter.31.cloned.1.call-start = ((), (), s32[]{:S(2)}) async-start(), calls=%async_computation.33 | async-start | bytes 4718592 | tf_op jit(solution)/shard_map/reduce_scatter | solution.py:267
  1273.6 219.3 %reduce-scatter.45.cloned.1.call-start = ((), (), s32[]{:S(2)}) async-start(), calls=%async_computation.41 | async-start | bytes 2359296 | tf_op jit(solution)/shard_map/reduce_scatter | solution.py:41
  1276.8 260.4 %reduce-scatter.43.cloned.1.call-start = ((), (), s32[]{:S(2)}) async-start(), calls=%async_computation.40 | async-start | bytes 2359296 | tf_op jit(solution)/shard_map/reduce_scatter | solution.py:41
  1278.9 333.3 %reduce-scatter.53.cloned.1.call-start = ((), (), s32[]{:S(2)}) async-start(), calls=%async_computation.45 | async-start | bytes 9437184 | tf_op jit(solution)/shard_map/reduce_scatter | solution.py:53
  1284.7 402.3 %reduce-scatter.51.cloned.1.call-start = ((), (), s32[]{:S(2)}) async-start(), calls=%async_computation.44 | async-start | bytes 9437184 | tf_op jit(solution)/shard_map/reduce_scatter | solution.py:53
  1292.1 470.0 %reduce-scatter.49.cloned.1.call-start = ((), (), s32[]{:S(2)}) async-start(), calls=%async_computation.43 | async-start | bytes 9437184 | tf_op jit(solution)/shard_map/reduce_scatter | solution.py:50
  1299.5 537.5 %reduce-scatter.47.cloned.1.call-start = ((), (), s32[]{:S(2)}) async-start(), calls=%async_computation.42 | async-start | bytes 9437184 | tf_op jit(solution)/shard_map/reduce_scatter | solution.py:50
  1306.6 34.5 %copy-start.6 = (bf16[2,1,128,1024]{3,2,1,0:T(8,128)(2,1)S(1)}, bf16[2,1,128,1024]{3,2,1,0:T(8,128)(2,1)}, u32[]{:S(2)}) copy-start(bf16[2,1,128,1024]{3,2,1,0:T(8,128)(2,1)} %param.13) | copy-start | bytes 1572868
  1306.6 34.5 %copy-start.41 = (f32[8,1,128]{2,1,0:T(1,128)S(1)}, f32[8,1,128]{2,1,0:T(1,128)}, u32[]{:S(2)}) copy-start(f32[8,1,128]{2,1,0:T(1,128)} %copy-done.40) | copy-start | bytes 12292
  1306.6 34.5 %copy-start.58 = (f32[128]{0:T(128)S(1)}, f32[128]{0:T(128)}, u32[]{:S(2)}) copy-start(f32[128]{0:T(128)} %copy-done.57) | copy-start | bytes 1540
  1306.6 34.5 %copy-start.64 = (f32[128]{0:T(128)S(1)}, f32[128]{0:T(128)}, u32[]{:S(2)}) copy-start(f32[128]{0:T(128)} %copy-done.63) | copy-start | bytes 1540
  1306.7 595.6 %reduce-scatter.41.cloned.1.call-start = ((), (), s32[]{:S(2)}) async-start(), calls=%async_computation.39 | async-start | bytes 7077888 | tf_op jit(solution)/shard_map/reduce_scatter | solution.py:38
  1345.8 104.0 %copy-start.56 = (f32[128]{0:T(128)S(1)}, f32[128]{0:T(128)}, u32[]{:S(2)}) copy-start(f32[128]{0:T(128)} %copy-done.55) | copy-start | bytes 1540
  1345.8 104.0 %copy-start.62 = (f32[128]{0:T(128)S(1)}, f32[128]{0:T(128)}, u32[]{:S(2)}) copy-start(f32[128]{0:T(128)} %copy-done.61) | copy-start | bytes 1540
  1345.8 621.4 %reduce-scatter.39.cloned.1.call-start = ((), (), s32[]{:S(2)}) async-start(), calls=%async_computation.38 | async-start | bytes 7077888 | tf_op jit(solution)/shard_map/reduce_scatter | solution.py:38
  1395.4 58.9 %copy-start.43 = (bf16[128,16,64]{0,2,1:T(8,128)(2,1)}, bf16[128,16,64]{0,2,1:T(8,128)(2,1)S(1)}, u32[]{:S(2)}) copy-start(bf16[128,16,64]{0,2,1:T(8,128)(2,1)S(1)} %convert.30) | copy-start | bytes 786436
  1454.4 549.6 %reduce-scatter.57.cloned.1.call-start = ((), (), s32[]{:S(2)}) async-start(), calls=%async_computation.47 | async-start | bytes 294912
  1472.4 568.2 %reduce-scatter.55.cloned.1.call-start = ((), (), s32[]{:S(2)}) async-start(), calls=%async_computation.46 | async-start | bytes 294912
  1473.6 691.8 %all-reduce.15.cloned.1.call-start = ((), (), s32[]{:S(2)}) async-start(), calls=%async_computation.48 | async-start | bytes 6291456 | tf_op jit(solution)/shard_map/psum | solution.py:290
  2046.4 33.1 %copy-start.26 = (f32[128,1024]{1,0:T(8,128)S(1)}, f32[128,1024]{1,0:T(8,128)}, u32[]{:S(2)}) copy-start(f32[128,1024]{1,0:T(8,128)} %copy-done.25) | copy-start | bytes 1572868
  2046.4 33.1 %copy-start.28 = (f32[128,1024]{1,0:T(8,128)S(1)}, f32[128,1024]{1,0:T(8,128)}, u32[]{:S(2)}) copy-start(f32[128,1024]{1,0:T(8,128)} %copy-done.27) | copy-start | bytes 1572868
  2046.5 33.1 %copy-start.91 = (f32[128]{0:T(128)S(1)}, f32[128]{0:T(128)}, u32[]{:S(2)}) copy-start(f32[128]{0:T(128)} %copy-done.90) | copy-start | bytes 1540
  2046.5 33.1 %copy-start.93 = (f32[128]{0:T(128)S(1)}, f32[128]{0:T(128)}, u32[]{:S(2)}) copy-start(f32[128]{0:T(128)} %copy-done.92) | copy-start | bytes 1540
  (77 other events, 475.5 us)
Sparse Core Ops, SparseCore 0:
  9.9 48.1 all-gather.14
  64.7 28.0 all-gather.18
  95.3 28.0 all-gather.16
  125.2 27.7 all-gather.20
  155.3 28.0 all-gather.30
  185.8 28.0 all-gather.28
  215.8 54.2 all-gather.22
  272.0 54.2 all-gather.24
  328.7 36.5 all-gather.32
  367.7 36.5 all-gather.26
  406.8 36.5 all-gather.36
  445.2 36.5 all-gather.34
  1235.6 50.0 reduce-scatter.36
  1288.9 51.0 reduce-scatter.34
  1343.2 51.0 reduce-scatter.32
  1397.6 51.0 reduce-scatter.30
  1451.8 41.1 reduce-scatter.44
  1496.1 41.0 reduce-scatter.42
  1540.7 71.5 reduce-scatter.52
  1615.5 71.5 reduce-scatter.50
  1690.5 71.5 reduce-scatter.48
  1765.6 71.4 reduce-scatter.46
  1840.5 61.6 reduce-scatter.40
  1905.4 61.7 reduce-scatter.38
  1970.2 33.6 reduce-scatter.56
  2006.8 33.6 reduce-scatter.54
  2044.1 121.2 all-reduce.14
where the time goes:
time: 2190 us; the launch traced here: 2180 us
  waiting for transfers between devices  1030 us (47%)
  blocking collectives  758 us (35%)
  matrix products  265 us (12%)
  other arithmetic  43.3 us (2%)
  local copies, waits for them, and re-layouts  42.6 us (2%)
  starting transfers between devices  22.1 us (1%)
    unnamed x2, blocking collectives  663 us
    reduce_scatter x2, waiting for transfers between devices, reduce_grads(): lax.psum_scatter(grad_down.astype(jnp.bfloat16), 'shard', scatter_dimensi...  148 us
    reduce_scatter x2, waiting for transfers between devices, reduce_grads(): lax.psum_scatter(grad_in.astype(jnp.bfloat16), 'shard', scatter_dimension...  147 us
    reduce_scatter x2, waiting for transfers between devices, reduce_grads(): lax.psum_scatter(grad_qkv.astype(jnp.bfloat16), 'shard', scatter_dimensio...  127 us
    psum x1, waiting for transfers between devices, per_device(): lax.psum(grads_acc[1].astype(jnp.bfloat16), 'expert').astype(jnp.float32)  84.5 us
    reduce_scatter x2, waiting for transfers between devices, per_device(): lax.psum_scatter(grad_keys_part, 'shard', scatter_dimension=0, tiled=True)  81 us
    unnamed x29, waiting for transfers between devices  63.7 us
    reduce_scatter x2, waiting for transfers between devices, reduce_grads(): lax.psum_scatter(grad_attn.astype(jnp.bfloat16), 'shard', scatter_dimensi...  63.3 us
  transfers between devices with their start and end apart: 32, of which 30 were waited for; matrix products, arithmetic and copies ran while one was open for 13% of the time, Pallas kernels for 0%

commit v1 on v0

v1 whole, which is shorter than its diff:
```python
import functools

import jax
import jax.numpy as jnp
import numpy as np
from jax import lax
from jax.experimental import pallas as pl
from jax.experimental.pallas import tpu as pltpu
from jax.sharding import PartitionSpec as P

HEADS = 16
HEAD_DIM = 64
F32 = jnp.float32
BF16 = jnp.bfloat16
GELU_A = 0.7978845608028654
GELU_B = 0.044715


def layer_norm(values, gain):
    center = jnp.mean(values, axis=-1, keepdims=True)
    shifted = values - center
    spread = jnp.mean(shifted * shifted, axis=-1, keepdims=True)
    return shifted * lax.rsqrt(spread + 1e-05) * gain


def bit_order(half, n):
    bits = [1 << i for i in range(n.bit_length() - 1)]
    rest = bits[1:]
    return (rest if half % 2 == 0 else rest[::-1]) + bits[:1]


def offsets(half, n):
    order = bit_order(half, n)
    return [sum(b for s, b in enumerate(order) if j >> s & 1) for j in range(n)]


def swap(x, bit, n):
    return lax.ppermute(x, "shard", [(i, i ^ bit) for i in range(n)])


def gather_rows(halves, n):
    held = list(halves)
    steps = n.bit_length() - 1
    for step in range(steps):
        got = [swap(x, bit_order(h, n)[step], n) for h, x in enumerate(held)]
        if step == steps - 1:
            return jnp.concatenate([y for pair in zip(held, got) for y in pair], axis=0)
        held = [jnp.concatenate(pair, axis=0) for pair in zip(held, got)]
    return jnp.concatenate(held, axis=0)


def scatter_sum(halves, n):
    held = list(halves)
    steps = n.bit_length() - 1
    for step in reversed(range(steps)):
        nxt = []
        for h, x in enumerate(held):
            size = x.shape[0] // 2
            got = swap(x[size:], bit_order(h, n)[step], n)
            nxt.append((x[:size].astype(F32) + got.astype(F32)).astype(BF16))
        held = nxt
    return held


def natural(order_ref, src_ref, dst_ref, n, rows):
    m = pl.program_id(0)
    for i in range(n):
        at = pl.multiple_of(order_ref[m, i] * rows, rows)
        dst_ref[i * rows : (i + 1) * rows, :] = src_ref[0, pl.ds(at, rows), :]


def of_head(x, h):
    lane = lax.broadcasted_iota(jnp.int32, x.shape, 1)
    return jnp.where(lane // HEAD_DIM == h, x, jnp.zeros_like(x))


def dot(a, b, ca, cb):
    return lax.dot_general(a, b, (((ca,), (cb,)), ((), ())), preferred_element_type=F32)


def attend_body(n, rows, hd, bq, order_ref, qkv_ref, segr_ref, segc_ref, out_ref, qkv_s):
    natural(order_ref, qkv_ref, qkv_s, n, rows)
    scale = HEAD_DIM ** (-0.5)
    for b in range(n * rows // bq):
        lo, hi = b * bq, (b + 1) * bq
        q, k, v = qkv_s[lo:hi, :hd], qkv_s[:hi, hd : 2 * hd], qkv_s[:hi, 2 * hd :]
        qpos = lo + lax.broadcasted_iota(jnp.int32, (bq, hi), 0)
        kpos = lax.broadcasted_iota(jnp.int32, (bq, hi), 1)
        allowed = (kpos <= qpos) & (segc_ref[0, lo:hi, :] == segr_ref[0, :, :hi])
        out = jnp.zeros((bq, hd), F32)
        for h in range(hd // HEAD_DIM):
            scores = dot(of_head(q, h), k, 1, 1) * scale
            top = jnp.max(jnp.where(allowed, scores, -1e30), axis=1, keepdims=True)
            e = jnp.where(allowed, jnp.exp(scores - top), 0.0)
            p = e / jnp.sum(e, axis=1, keepdims=True)
            out = out + of_head(dot(p.astype(BF16), v, 1, 0), h)
        out = out.astype(BF16)
        for i in range(bq // rows):
            out_ref[lo // rows + i, 0] = out[i * rows : (i + 1) * rows, :]


def attend_back_body(
    n, rows, hd, bq, order_ref, qkv_ref, go_ref, segr_ref, segc_ref, out_ref, qkv_s, acc_s
):
    natural(order_ref, qkv_ref, qkv_s, n, rows)
    m = pl.program_id(0)
    scale = HEAD_DIM ** (-0.5)
    acc_s[...] = jnp.zeros_like(acc_s)
    for b in range(n * rows // bq):
        lo, hi = b * bq, (b + 1) * bq
        q, k, v = qkv_s[lo:hi, :hd], qkv_s[:hi, hd : 2 * hd], qkv_s[:hi, 2 * hd :]
        go = jnp.concatenate([go_ref[lo // rows + i, 0] for i in range(bq // rows)], axis=0)
        kpos = lax.broadcasted_iota(jnp.int32, (hi, bq), 0)
        qpos = lo + lax.broadcasted_iota(jnp.int32, (hi, bq), 1)
        allowed = (kpos <= qpos) & (segc_ref[0, :hi, :] == segr_ref[0, :, lo:hi])
        dq = jnp.zeros((bq, hd), F32)
        dk = jnp.zeros((hi, hd), F32)
        dv = jnp.zeros((hi, hd), F32)
        for h in range(hd // HEAD_DIM):
            scores = dot(k, of_head(q, h), 1, 1) * scale
            top = jnp.max(jnp.where(allowed, scores, -1e30), axis=0, keepdims=True)
            e = jnp.where(allowed, jnp.exp(scores - top), 0.0)
            p = e / jnp.sum(e, axis=0, keepdims=True)
            dp = dot(v, of_head(go, h), 1, 1)
            delta = jnp.sum(p * dp, axis=0, keepdims=True)
            ds = (p * (dp - delta)).astype(BF16)
            dq = dq + of_head(dot(ds, k, 0, 0), h)
            dk = dk + of_head(dot(ds, q, 1, 0), h)
            dv = dv + of_head(dot(p.astype(BF16), go, 1, 0), h)
        acc_s[lo:hi, :hd] = dq * scale
        acc_s[:hi, hd : 2 * hd] += dk * scale
        acc_s[:hi, 2 * hd :] += dv
    for i in range(n):
        at = pl.multiple_of(order_ref[m, i] * rows, rows)
        out_ref[0, pl.ds(at, rows), :] = acc_s[i * rows : (i + 1) * rows, :].astype(BF16)


def attend(order, qkv, segments, n, rows, hd, grad_heads=None):
    micro, seq, cols = qkv.shape
    segr, segc = segments[:, None, :], segments[:, :, None]
    bq = min(seq, 256)
    flat = pl.BlockSpec((1, seq, cols), lambda m, o: (m, 0, 0))
    heads = pl.BlockSpec((n, 1, rows, hd), lambda m, o: (0, m, 0, 0))
    segs = [
        pl.BlockSpec((1, 1, seq), lambda m, o: (m, 0, 0)),
        pl.BlockSpec((1, seq, 1), lambda m, o: (m, 0, 0)),
    ]
    scratch = [pltpu.VMEM((seq, cols), BF16)]
    area = micro * seq * seq * (hd // HEAD_DIM)
    if grad_heads is None:
        return pl.pallas_call(
            functools.partial(attend_body, n, rows, hd, bq),
            out_shape=jax.ShapeDtypeStruct((n, micro, rows, hd), BF16),
            grid_spec=pltpu.PrefetchScalarGridSpec(
                num_scalar_prefetch=1,
                grid=(micro,),
                in_specs=[flat] + segs,
                out_specs=heads,
                scratch_shapes=scratch,
            ),
            name="attend",
            cost_estimate=pl.CostEstimate(
                flops=area * 512, transcendentals=area, bytes_accessed=qkv.size * 3
            ),
        )(order, qkv, segr, segc)
    return pl.pallas_call(
        functools.partial(attend_back_body, n, rows, hd, bq),
        out_shape=jax.ShapeDtypeStruct((micro, seq, cols), BF16),
        grid_spec=pltpu.PrefetchScalarGridSpec(
            num_scalar_prefetch=1,
            grid=(micro,),
            in_specs=[flat, heads] + segs,
            out_specs=flat,
            scratch_shapes=scratch + [pltpu.VMEM((seq, cols), F32)],
        ),
        name="attend_back",
        cost_estimate=pl.CostEstimate(
            flops=area * 1280, transcendentals=area, bytes_accessed=qkv.size * 6
        ),
    )(order, qkv, grad_heads, segr, segc)


def ffn_body(branch, x_ref, c_ref, wi_ref, wo_ref, wm_ref, yd_ref, gi_ref, go_ref):
    width = x_ref.shape[1]
    x = x_ref[...]
    wi, wo = wi_ref[...], wo_ref[...]
    logits = dot(x, wm_ref[...], 1, 0)
    first, second = logits[:, 0:1], logits[:, 1:2]
    top = jnp.maximum(first, second)
    first, second = jnp.exp(first - top), jnp.exp(second - top)
    mix = (second if branch else first) / (first + second)
    g = (mix * c_ref[...].astype(F32)).astype(BF16)
    up = dot(x, wi, 1, 0)
    t = jnp.tanh(GELU_A * (up + GELU_B * (up * up * up)))
    act = (0.5 * up * (1.0 + t)).astype(BF16)
    slope = 0.5 * (1.0 + t) + 0.5 * up * (1.0 - t * t) * (GELU_A * (1.0 + 3.0 * GELU_B * up * up))
    yd_ref[:, :width] = dot(act, wo, 1, 0).astype(BF16)
    dup = (dot(g, wo, 1, 1) * slope).astype(BF16)
    yd_ref[:, width:] = dot(dup, wi, 1, 1).astype(BF16)
    gi = dot(x, dup, 0, 0)
    go = dot(act, g, 0, 0)

    @pl.when(pl.program_id(0) == 0)
    def _():
        gi_ref[...] = gi
        go_ref[...] = go

    @pl.when(pl.program_id(0) > 0)
    def _():
        gi_ref[...] += gi
        go_ref[...] += go


def ffn(branch, x, c, w_in, w_out, mix_pad):
    count, width = x.shape
    units = w_in.shape[1]
    block = min(count, 512)
    row = lambda cols: pl.BlockSpec((block, cols), lambda b: (b, 0))
    whole = lambda a: pl.BlockSpec(a, lambda b: (0, 0))
    return pl.pallas_call(
        functools.partial(ffn_body, branch),
        out_shape=(
            jax.ShapeDtypeStruct((count, 2 * width), BF16),
            jax.ShapeDtypeStruct((width, units), F32),
            jax.ShapeDtypeStruct((units, width), F32),
        ),
        grid=(count // block,),
        in_specs=[
            row(width),
            row(width),
            whole(w_in.shape),
            whole(w_out.shape),
            whole(mix_pad.shape),
        ],
        out_specs=(row(2 * width), whole(w_in.shape), whole(w_out.shape)),
        name="ffn",
        compiler_params=pltpu.CompilerParams(vmem_limit_bytes=56 * 1024 * 1024),
        cost_estimate=pl.CostEstimate(
            flops=12 * count * width * units,
            transcendentals=count * units,
            bytes_accessed=8 * count * width + 12 * width * units,
        ),
    )(x, c, w_in, w_out, mix_pad)


def per_device(
    tokens,
    segments,
    routes,
    cotangent,
    norm1_gain,
    qkv_weight,
    out_weight,
    norm2_gain,
    mix_weight,
    dense_in,
    dense_out,
    expert_in,
    expert_out,
):
    highest = lax.Precision.HIGHEST
    micro, _, rows, width = tokens.shape
    n = lax.axis_size("shard")
    n_expert = lax.axis_size("expert")
    me = lax.axis_index("shard")
    seq = segments.shape[2]
    hd = width // n
    local = expert_in.shape[0]
    experts = local * n_expert
    capacity = max(2, 2 * rows // experts)
    wrow = qkv_weight.shape[0]
    segs = segments[:, 0]
    x_in = tokens[:, 0]
    cot = cotangent[:, 0]
    table = np.array(
        [[[offsets(m, n).index(i ^ d) for i in range(n)] for m in range(micro)] for d in range(n)],
        np.int32,
    )
    order = jnp.asarray(table)[me]

    tokens_all = gather_rows([x_in[m] for m in range(micro)], n)
    small = jnp.concatenate([norm1_gain[None], norm2_gain[None], mix_weight.T], axis=0)
    small_all = lax.all_gather(small, "shard", axis=0).transpose(1, 0, 2).reshape(4, width)
    gain_one, gain_two = small_all[0].astype(F32), small_all[1].astype(F32)
    mix_full = small_all[2:].T
    mix_pad = jnp.pad(mix_full, ((0, 0), (0, 126)))
    wq = qkv_weight.reshape(wrow, 3, n, hd).transpose(2, 0, 1, 3).reshape(n, wrow, 3 * hd)
    wq = lax.all_to_all(wq, "shard", split_axis=0, concat_axis=0, tiled=True)
    wq = wq.reshape(width, 3 * hd)
    wo_full = lax.all_gather(out_weight, "shard", axis=0, tiled=True)
    units = dense_in.shape[1] // n
    w_in = dense_in.reshape(wrow, n, units).transpose(1, 0, 2)
    w_in = lax.all_to_all(w_in, "shard", split_axis=0, concat_axis=0, tiled=True)
    w_in = w_in.reshape(width, units)

    route = routes[:, 0, :, 0]
    onehot = (route[:, :, None] == jnp.arange(experts, dtype=jnp.int32)).astype(jnp.int32)
    rank = jnp.sum((jnp.cumsum(onehot, axis=1) - onehot) * onehot, axis=2)
    slot = route * capacity + rank
    slot_ids = jnp.arange(experts * capacity, dtype=jnp.int32)
    placing = (slot[:, None, :] == slot_ids[None, :, None]).astype(BF16)

    def dispatch(values):
        sent = jnp.einsum("mst,mtd->msd", placing, values, preferred_element_type=F32).astype(BF16)
        sent = sent.reshape(micro, n_expert, local, capacity, width).transpose(1, 2, 0, 3, 4)
        got = lax.all_to_all(sent, "expert", split_axis=0, concat_axis=0, tiled=True)
        got = got.transpose(1, 2, 0, 3, 4).reshape(local, micro, n_expert * capacity, width)
        return [gather_rows([got[j, m] for m in range(micro)], n) for j in range(local)]

    cot_all = gather_rows([cot[m] for m in range(micro)], n)
    cot_rows = dispatch(cot)

    wide = tokens_all.astype(F32)
    center = jnp.mean(wide, axis=-1, keepdims=True)
    shifted = wide - center
    spread = jnp.mean(shifted * shifted, axis=-1, keepdims=True)
    unit_all = shifted * lax.rsqrt(spread + 1e-05)
    normed_all = (unit_all * gain_one).astype(BF16)
    qkv = jnp.dot(normed_all, wq, preferred_element_type=F32).astype(BF16)
    qkv = qkv.reshape(micro, seq, 3 * hd)
    heads = attend(order, qkv, segs, n, rows, hd)
    heads = lax.all_to_all(heads, "shard", split_axis=0, concat_axis=0, tiled=True)
    heads_out = heads.transpose(1, 2, 0, 3).reshape(micro * rows, width)
    inputs = x_in.reshape(micro * rows, width).astype(F32)
    mid = inputs + jnp.dot(heads_out, wo_full, preferred_element_type=F32)

    normed_t, norm_two_back = jax.vjp(layer_norm, mid, gain_two)
    normed_two = normed_t.astype(BF16)
    by_half = normed_two.reshape(micro, rows, width)
    x_all = gather_rows([by_half[m] for m in range(micro)], n)
    x_rows = dispatch(by_half)

    def split(values):
        return [values[m * (values.shape[0] // micro) :][: values.shape[0] // micro] for m in range(micro)]

    part, in_grad, down_grad = ffn(0, x_all, cot_all, w_in, dense_out, mix_pad)
    dense_sum = jnp.concatenate(scatter_sum(split(part), n), axis=0).astype(F32)
    in_grad = in_grad.reshape(n, wrow, units).astype(BF16)
    in_grad = lax.all_to_all(in_grad, "shard", split_axis=0, concat_axis=0, tiled=True)
    in_grad = in_grad.transpose(1, 0, 2).reshape(wrow, n * units)
    in_total = lax.psum(in_grad, "expert").astype(F32)
    down_total = lax.psum(down_grad.astype(BF16), "expert").astype(F32)

    sums, e_in_grads, e_out_grads = [], [], []
    for j in range(local):
        part, gi, go = ffn(1, x_rows[j], cot_rows[j], expert_in[j], expert_out[j], mix_pad)
        sums.append(jnp.stack(scatter_sum(split(part), n)))
        e_in_grads.append(gi)
        e_out_grads.append(go)
    back = jnp.stack(sums).reshape(local, micro, n_expert, capacity, 2 * width)
    back = lax.all_to_all(
        back.transpose(2, 0, 1, 3, 4), "expert", split_axis=0, concat_axis=0, tiled=True
    )
    back = back.transpose(2, 0, 1, 3, 4).reshape(micro, experts * capacity, 2 * width)
    expert_sum = jnp.einsum("mst,msd->mtd", placing, back, preferred_element_type=F32)
    expert_sum = expert_sum.reshape(micro * rows, 2 * width)

    logits = jnp.dot(normed_two, mix_full, preferred_element_type=F32)
    mixing, mixing_back = jax.vjp(lambda values: jax.nn.softmax(values, axis=-1), logits)
    dense_branch, expert_branch = dense_sum[:, :width], expert_sum[:, :width]
    output = (mid + mixing[:, 0:1] * dense_branch + mixing[:, 1:2] * expert_branch).astype(BF16)
    grad_y = cot.reshape(micro * rows, width).astype(F32)
    grad_mix_c = jnp.stack(
        [jnp.sum(grad_y * dense_branch, axis=-1), jnp.sum(grad_y * expert_branch, axis=-1)],
        axis=-1,
    )
    grad_logits = mixing_back(grad_mix_c)[0]
    grad_mix = jnp.einsum("td,tc->dc", normed_two.astype(F32), grad_logits, precision=highest)
    grad_normed_two = (
        dense_sum[:, width:]
        + expert_sum[:, width:]
        + jnp.einsum("tc,dc->td", grad_logits, mix_full.astype(F32), precision=highest)
    )
    grad_mid_norm, grad_two = norm_two_back(grad_normed_two)
    grad_mid = grad_y + grad_mid_norm

    grad_attn = grad_mid.astype(BF16)
    grad_heads = jnp.einsum("te,de->td", grad_attn, wo_full, preferred_element_type=F32)
    grad_heads = grad_heads.astype(BF16).reshape(micro, rows, n, hd).transpose(2, 0, 1, 3)
    grad_heads = lax.all_to_all(grad_heads, "shard", split_axis=0, concat_axis=0, tiled=True)
    grad_wo = jnp.einsum("td,te->de", heads_out, grad_attn, preferred_element_type=F32)
    tail = jnp.concatenate([grad_two[None], grad_mix.T], axis=0).reshape(3, n, wrow)
    tail = tail.transpose(1, 0, 2).reshape(n, 1, 3 * wrow)
    tail = jnp.pad(tail, ((0, 0), (0, 15), (0, width - 3 * wrow)))
    grad_wo = jnp.concatenate([grad_wo.reshape(n, wrow, width), tail], axis=1).astype(BF16)
    grad_wo = lax.psum_scatter(grad_wo, "shard", scatter_dimension=0, tiled=True)[0]

    grad_qkv = attend(order, qkv, segs, n, rows, hd, grad_heads).reshape(micro * seq, 3 * hd)
    grad_normed_one = jnp.einsum("te,de->td", grad_qkv, wq, preferred_element_type=F32)
    gain_one_part = jnp.sum(grad_normed_one * unit_all, axis=0)
    first = scatter_sum(split(grad_normed_one.astype(BF16)), n)
    first = jnp.concatenate(first, axis=0).astype(F32)
    _, norm_one_back = jax.vjp(lambda v: layer_norm(v, gain_one), inputs)
    input_grad = (grad_mid + norm_one_back(first)[0]).astype(BF16)
    grad_wq = jnp.einsum("td,te->de", normed_all, grad_qkv, preferred_element_type=F32)
    grad_wq = grad_wq.reshape(n, wrow, 3 * hd)
    ones = jnp.pad(gain_one_part.reshape(n, 1, wrow), ((0, 0), (0, 15), (0, 3 * hd - wrow)))
    grad_wq = jnp.concatenate([grad_wq, ones], axis=1).astype(BF16)
    grad_wq = lax.all_to_all(grad_wq, "shard", split_axis=0, concat_axis=0, tiled=True)
    gain_one_grad = jnp.sum(grad_wq[:, wrow, :wrow].astype(F32), axis=0)
    grad_wq = grad_wq[:, :wrow].reshape(n, wrow, 3, hd).transpose(1, 2, 0, 3)
    grad_wq = grad_wq.reshape(wrow, 3 * width)

    wq_total = lax.psum(grad_wq, "expert").astype(F32)
    wo_total = lax.psum(grad_wo[:wrow], "expert").astype(F32)
    vectors = jnp.concatenate([grad_wo[wrow, : 3 * wrow].astype(F32), gain_one_grad])
    vectors = lax.psum(vectors, "expert").reshape(4, wrow)

    return (
        output.reshape(micro, 1, rows, width),
        input_grad.reshape(micro, 1, rows, width),
        vectors[3],
        wq_total,
        wo_total,
        vectors[0],
        vectors[1:3].T,
        in_total,
        down_total,
        jnp.stack(e_in_grads),
        jnp.stack(e_out_grads),
    )


def solution(mesh):
    return jax.shard_map(
        per_device,
        mesh=mesh,
        in_specs=(
            P(None, "expert", "shard", None),
            P(None, "expert", None),
            P(None, "expert", "shard", None),
            P(None, "expert", "shard", None),
            P("shard"),
            P("shard", None),
            P("shard", None),
            P("shard"),
            P("shard", None),
            P("shard", None),
            P("shard", None),
            P("expert", None, "shard"),
            P("expert", "shard", None),
        ),
        out_specs=(
            P(None, "expert", "shard", None),
            P(None, "expert", "shard", None),
            P("shard"),
            P("shard", None),
            P("shard", None),
            P("shard"),
            P("shard", None),
            P("shard", None),
            P("shard", None),
            P("expert", None, "shard"),
            P("expert", "shard", None),
        ),
        check_vma=False,
    )
```

time: 2190 us -> 776 us (0.35)
  waiting for transfers between devices: 1030 us -> 256 us
  blocking collectives: 758 us -> 28.5 us
  matrix products: 265 us -> 24.3 us
  Pallas kernels: 0 us -> 100 us
  local copies, waits for them, and re-layouts: 42.6 us -> 142 us
  starting transfers between devices: 22.1 us -> 101 us
  other arithmetic: 43.3 us -> 103 us
    unnamed x2 -> x0, blocking collectives: 663 us -> none
    reduce_scatter x12 -> x1, waiting for transfers between devices: 611 us -> 0.01 us  [per_device(): lax.psum_scatter(grad_wo, 'shard', scatter_dimension=0, tiled=True)[0]]
    all_gather x12 -> x1, waiting for transfers between devices: 234 us -> 0.01 us  [per_device(): wo_full = lax.all_gather(out_weight, 'shard', axis=0, tiled=True)]
    dot_general x60 -> x12, matrix products: 245 us -> 24.3 us  [the longest x1 6.3 us: per_device(): jnp.einsum('te,de->td', grad_qkv, wq, preferred_element_type=F32)]
    ppermute x0 -> x66, waiting for transfers between devices: none -> 153 us  [swap(): return lax.ppermute(x, 'shard', [(i, i ^ bit) for i in range(n)])]
    pallas_call x0 -> x5, Pallas kernels: none -> 100 us  [the longest x3 70.7 us: ffn(): pl.pallas_call(functools.partial(ffn_body, branch), out_shape=(jax.ShapeD...]
    unnamed x29 -> x3, waiting for transfers between devices: 63.7 us -> 0.71 us
    ppermute x0 -> x66, starting transfers between devices: none -> 61.3 us  [swap(): return lax.ppermute(x, 'shard', [(i, i ^ bit) for i in range(n)])]
  transfers between devices with their start and end apart: 32 -> 78, of which waited for: 30 -> 26; matrix products, arithmetic and copies ran while one was open for 13% -> 32% of each run, Pallas kernels for 0% -> 13%
where the time goes in v1:
time: 776 us; the launch traced here: 770 us
  waiting for transfers between devices  256 us (33%)
  local copies, waits for them, and re-layouts  142 us (18%)
  other arithmetic  103 us (13%)
  starting transfers between devices  101 us (13%)
  Pallas kernels  100 us (13%)
  blocking collectives  28.5 us (4%)
  matrix products  24.3 us (3%)
  between operations  15.5 us (2%)
    ppermute x66, waiting for transfers between devices, swap(): return lax.ppermute(x, 'shard', [(i, i ^ bit) for i in range(n)])  153 us
    psum x1, waiting for transfers between devices, per_device(): wq_total = lax.psum(grad_wq, 'expert').astype(F32)  90.7 us
    pallas_call x3, Pallas kernels, ffn(): pl.pallas_call(functools.partial(ffn_body, branch), out_shape=(jax.ShapeD...  70.7 us
    unnamed x171, local copies, waits for them, and re-layouts  62.7 us
    ppermute x66, starting transfers between devices, swap(): return lax.ppermute(x, 'shard', [(i, i ^ bit) for i in range(n)])  61.3 us
    concatenate x28, other arithmetic, gather_rows(): held = [jnp.concatenate(pair, axis=0) for pair in zip(held, got)]  40.4 us
    convert_element_type x20, other arithmetic, scatter_sum(): nxt.append((x[:size].astype(F32) + got.astype(F32)).astype(BF16))  28.7 us
    slice x20, local copies, waits for them, and re-layouts, scatter_sum(): got = swap(x[size:], bit_order(h, n)[step], n)  21.1 us
  transfers between devices with their start and end apart: 78, of which 26 were waited for; matrix products, arithmetic and copies ran while one was open for 32% of the time, Pallas kernels for 13%

profile of v1, /device:TPU:0, one launch (start us, length us, event | category | flops | bytes accessed | tf_op | source)
XLA Modules:
  0.0 770.5 jit_solution(11668800323316987723)
XLA Ops:
  9.2 3.0 collective-permute-start
  16.1 3.5 all-to-all-start
  25.4 18.0 %all-gather.1 = bf16[8,4,128]{2,1,0:T(4,128)(2,1)S(1)} all-gather(bf16[1,4,128]{2,1,0:T(4,128)(2,1)S(1)} %maximum_bitcast_fusion.2), channel_id=2, replica_groups=mesh['shard'=8,'expert'=4] {'shard'}, dimensions={0}, use_global_device_ids=true | all-gather | bytes 9216 | tf_op jit(solution)/shard_map/all_gather | solution.py:283
  44.5 3.4 slice_bitcast_fusion.2
  52.0 5.3 all-to-all-start.4
  60.2 2.4 copy.135
  85.3 5.2 collective-permute-done.13
  112.7 2.9 convert_reduce_fusion
  115.6 3.0 fusion.6
  118.6 5.8 convolution_convert_fusion
  124.4 11.8 %attend.1 = bf16[8,2,128,128]{3,2,1,0:T(8,128)(2,1)} custom-call(s32[2,8]{1,0:T(2,128)} %dynamic-slice_bitcast_fusion.order_ref, bf16[2,1024,384]{2,1,0:T(8,128)(2,1)} %bitcast.320, s32[2,1,1024]{2,1,0:T(1,128)} %segr_ref.3, s32[2,1024,1]{2,1,0:T(8,128)} %broadcast_in_dim_squeeze.6.segc_ref), custom_call_target="tpu_custom_call" | custom-call | flops 2147483648 | bytes 2359296 | tf_op jit(solution)/shard_map/attend/pallas_call | solution.py:151
  136.2 4.4 all-to-all-start.1
  148.6 6.9 collective-permute-done.51
  160.8 2.3 constant_dynamic-update-slice_fusion.20
  163.8 2.9 collective-permute-done.31
  167.9 9.5 %collective-permute-done.49 = bf16[256,1024]{1,0:T(8,128)(2,1)S(1)} collective-permute-done((bf16[256,1024]{1,0:T(8,128)(2,1)S(1)}, bf16[256,1024]{1,0:T(8,128)(2,1)S(1)}, u32[]{:S(2)}, u32[]{:S(2)}) %collective-permute-start.49) | collective-permute-done | bytes 524320 | tf_op jit(solution)/shard_map/ppermute | solution.py:38
  182.2 2.3 constant_dynamic-update-slice_fusion.16.c_ref
  197.8 2.4 fusion.52
  202.4 4.9 all-to-all-start.3
  213.7 2.3 constant_dynamic-update-slice_fusion.32.c_ref
  215.9 2.3 collective-permute-done.9
  220.2 2.7 collective-permute-start.7
  225.6 2.3 constant_dynamic-update-slice_fusion.48.c_ref
  228.5 3.1 collective-permute-done.10
  234.5 4.3 all-to-all-start.2
  246.0 13.3 %collective-permute-done.42 = bf16[128,1024]{1,0:T(8,128)(2,1)S(1)} collective-permute-done((bf16[128,1024]{1,0:T(8,128)(2,1)S(1)}, bf16[128,1024]{1,0:T(8,128)(2,1)S(1)}, u32[]{:S(2)}, u32[]{:S(2)}) %collective-permute-start.42) | collective-permute-done | bytes 262176 | tf_op jit(solution)/shard_map/ppermute | solution.py:38
  261.7 2.7 collective-permute-done.24
  277.9 23.5 %ffn.3 = (bf16[2048,2048]{1,0:T(8,128)(2,1)}, f32[1024,512]{1,0:T(8,128)}, f32[512,1024]{1,0:T(8,128)}) custom-call(bf16[2048,1024]{1,0:T(8,128)(2,1)} %constant_dynamic-update-slice_fusion.8.x_ref, bf16[2048,1024]{1,0:T(8,128)(2,1)} %constant_dynamic-update-slice_fusion.16.c_ref, bf16[1024,512]{1,0:T(8,128)(2,1)} %bitcast.22.wi_ref, ...), custom_call_target="tpu_custom_call" | custom-call | flops 12884901888 | bytes 23068672 | tf_op jit(solution)/shard_map/ffn/pallas_call | solution.py:220
  304.3 4.9 fusion.45
  322.5 23.8 %ffn.4 = (bf16[2048,2048]{1,0:T(8,128)(2,1)}, f32[1024,512]{1,0:T(8,128)}, f32[512,1024]{1,0:T(8,128)}) custom-call(bf16[2048,1024]{1,0:T(8,128)(2,1)} %copy-done.53, bf16[2048,1024]{1,0:T(8,128)(2,1)} %constant_dynamic-update-slice_fusion.32.c_ref, bf16[1024,512]{1,0:T(8,128)(2,1)} %get-tuple-element.107.wi_ref, ...), custom_call_target="tpu_custom_call" | custom-call | flops 12884901888 | bytes 23068672 | tf_op jit(solution)/shard_map/ffn/pallas_call | solution.py:220
  346.2 4.1 fusion.46
  355.8 23.5 %ffn.5 = (bf16[2048,2048]{1,0:T(8,128)(2,1)}, f32[1024,512]{1,0:T(8,128)}, f32[512,1024]{1,0:T(8,128)}) custom-call(bf16[2048,1024]{1,0:T(8,128)(2,1)} %constant_dynamic-update-slice_fusion.40.x_ref, bf16[2048,1024]{1,0:T(8,128)(2,1)} %constant_dynamic-update-slice_fusion.48.c_ref, bf16[1024,512]{1,0:T(8,128)(2,1)} %get-tuple-element.108.wi_ref, ...), custom_call_target="tpu_custom_call" | custom-call | flops 12884901888 | bytes 23068672 | tf_op jit(solution)/shard_map/ffn/pallas_call | solution.py:220
  379.3 4.7 fusion.47
  387.6 5.8 add_convert_fusion.3
  395.1 7.8 %add_convert_fusion.5 = (bf16[512,2048]{1,0:T(8,128)(2,1)S(1)}, bf16[512,2048]{1,0:T(8,128)(2,1)}) fusion(bf16[512,2048]{1,0:T(8,128)(2,1)} %collective-permute-done.18, bf16[2048,2048]{1,0:T(8,128)(2,1)} %get-tuple-element.20, bf16[512,2048]{1,0:T(8,128)(2,1)} %collective-permute-done.21), kind=kLoop, calls=%fused_computation.18 | loop fusion | flops 8388608 | bytes 12582912 | tf_op jit(solution)/shard_map/convert_element_type | solution.py:60
  405.6 4.5 add_convert_fusion.1
  414.1 5.6 collective-permute-done.37
  420.5 11.0 %collective-permute-done.40 = bf16[256,2048]{1,0:T(8,128)(2,1)S(1)} collective-permute-done((bf16[256,2048]{1,0:T(8,128)(2,1)}, bf16[256,2048]{1,0:T(8,128)(2,1)S(1)}, u32[]{:S(2)}, u32[]{:S(2)}) %collective-permute-start.40) | collective-permute-done | bytes 1048608 | tf_op jit(solution)/shard_map/ppermute | solution.py:38
  433.9 30.6 %collective-permute-done.55 = bf16[256,2048]{1,0:T(8,128)(2,1)S(1)} collective-permute-done((bf16[256,2048]{1,0:T(8,128)(2,1)S(1)}, bf16[256,2048]{1,0:T(8,128)(2,1)S(1)}, u32[]{:S(2)}, u32[]{:S(2)}) %collective-permute-start.55) | collective-permute-done | bytes 1048608 | tf_op jit(solution)/shard_map/ppermute | solution.py:38
  467.8 8.0 %collective-permute-done.41 = bf16[128,2048]{1,0:T(8,128)(2,1)S(1)} collective-permute-done((bf16[128,2048]{1,0:T(8,128)(2,1)S(1)}, bf16[128,2048]{1,0:T(8,128)(2,1)S(1)}, u32[]{:S(2)}, u32[]{:S(2)}) %collective-permute-start.41) | collective-permute-done | bytes 524320 | tf_op jit(solution)/shard_map/ppermute | solution.py:38
  478.0 8.5 %collective-permute-done.59 = bf16[128,2048]{1,0:T(8,128)(2,1)S(1)} collective-permute-done((bf16[128,2048]{1,0:T(8,128)(2,1)S(1)}, bf16[128,2048]{1,0:T(8,128)(2,1)S(1)}, u32[]{:S(2)}, u32[]{:S(2)}) %collective-permute-start.59) | collective-permute-done | bytes 524320 | tf_op jit(solution)/shard_map/ppermute | solution.py:38
  488.1 4.7 all-to-all-start.5
  498.8 21.9 %collective-permute-done.22 = bf16[256,2048]{1,0:T(8,128)(2,1)S(1)} collective-permute-done((bf16[256,2048]{1,0:T(8,128)(2,1)S(1)}, bf16[256,2048]{1,0:T(8,128)(2,1)S(1)}, u32[]{:S(2)}, u32[]{:S(2)}) %collective-permute-start.22) | collective-permute-done | bytes 1048608 | tf_op jit(solution)/shard_map/ppermute | solution.py:38
  522.7 7.7 %collective-permute-done.20 = bf16[128,2048]{1,0:T(8,128)(2,1)S(1)} collective-permute-done((bf16[128,2048]{1,0:T(8,128)(2,1)S(1)}, bf16[128,2048]{1,0:T(8,128)(2,1)S(1)}, u32[]{:S(2)}, u32[]{:S(2)}) %collective-permute-start.20) | collective-permute-done | bytes 524320 | tf_op jit(solution)/shard_map/ppermute | solution.py:38
  533.9 7.1 all-to-all-done.5
  548.7 4.2 all-to-all-start.6
  555.3 2.7 convert_element_type.456
  558.0 4.6 all-to-all-done.6.go_ref
  562.6 3.8 all-to-all-start.8
  566.4 17.7 %attend_back.1 = bf16[2,1024,384]{2,1,0:T(8,128)(2,1)} custom-call(s32[2,8]{1,0:T(2,128)} %dynamic-slice_bitcast_fusion.order_ref, bf16[2,1024,384]{2,1,0:T(8,128)(2,1)} %bitcast.321, bf16[8,2,128,128]{3,2,1,0:T(8,128)(2,1)} %all-to-all-done.6.go_ref, s32[2,1,1024]{2,1,0:T(1,128)} %segr_ref.3, s32[2,1024,1]{2,1,0:T(8,128)} %broadcast_in_dim_squeeze.6.segc_ref), custom_call_target="tpu_custom_call" | custom-call | flops 5368709120 | bytes 4718592 | tf_op jit(solution)/shard_map/attend_back/pallas_call | solution.py:166
  584.2 6.3 fusion.5
  597.1 6.6 copy.117
  603.6 5.0 convolution_convert_fusion.4
  609.6 4.2 all-to-all-start.7
  614.3 3.3 add_convert_fusion.7
  621.3 2.4 pad_maximum_fusion.1
  626.1 2.5 pad_maximum_fusion
  630.6 2.3 copy.109
  643.4 3.9 collective-permute-done.62
  647.4 2.7 collective-permute-done.65
  653.2 10.5 %psum.35 = f32[512]{0:T(512)S(1)} all-reduce(f32[512]{0:T(512)S(1)} %pad_maximum_fusion.31), channel_id=1, replica_groups=mesh['shard'=8,'expert'=4] {'expert'}, use_global_device_ids=true, to_apply=%region_21.22 | all-reduce | flops 512 | bytes 4096 | tf_op jit(solution)/shard_map/psum | solution.py:407
  664.8 90.7 %all-reduce.6.cloned.1.call-done = (bf16[128,3072]{0,1:T(8,128)(2,1)}, bf16[128,1024]{1,0:T(8,128)(2,1)}, bf16[128,4096]{1,0:T(8,128)(2,1)}, bf16[512,1024]{1,0:T(8,128)(2,1)}) async-done(((bf16[128,3072]{0,1:T(8,128)(2,1)}, bf16[128,1024]{1,0:T(8,128)(2,1)}, bf16[128,4096]{1,0:T(8,128)(2,1)}, bf16[512,1024]{1,0:T(8,128)(2,1)}), (bf16[128,3072]{0,1:T(8,128)(2,1)}, bf16[128,1024]{1,0:T(8,128)(2,1)}, ...) | async-done | bytes 3145744 | tf_op jit(solution)/shard_map/psum | solution.py:404
  755.5 2.8 convert_element_type.458
  758.4 2.8 convert_element_type.460
  (444 shorter events, 235.2 us)
Async XLA Ops:
  9.2 54.1 %collective-permute-start = (bf16[128,1024]{1,0:T(8,128)(2,1)}, bf16[128,1024]{1,0:T(8,128)(2,1)}, u32[]{:S(2)}, u32[]{:S(2)}) collective-permute-start(bf16[128,1024]{1,0:T(8,128)(2,1)} %get-tuple-element.131), channel_id=1, source_target_pairs={{0,8},{4,12},{8,0},{12,4},{16,24},{20,28},{24,16},{28,20},{1,9},{5... | collective-permute-start | bytes 786440 | tf_op jit(solution)/shard_map/ppermute | solution.py:38
  12.1 53.3 %collective-permute-start.3 = (bf16[128,1024]{1,0:T(8,128)(2,1)}, bf16[128,1024]{1,0:T(8,128)(2,1)}, u32[]{:S(2)}, u32[]{:S(2)}) collective-permute-start(bf16[128,1024]{1,0:T(8,128)(2,1)} %get-tuple-element.130), channel_id=1, source_target_pairs={{0,16},{4,20},{8,24},{12,28},{16,0},{20,4},{24,8},{28,12},{1,17},{... | collective-permute-start | bytes 786440 | tf_op jit(solution)/shard_map/ppermute | solution.py:38
  16.1 35.0 %all-to-all-start = ((bf16[8,128,384]{1,2,0:T(8,128)(2,1)}), bf16[8,128,384]{1,2,0:T(8,128)(2,1)S(1)}, u32[]{:S(2)}, u32[]{:S(2)}) async-start(bf16[8,128,384]{1,2,0:T(8,128)(2,1)} %bitcast.12), calls=%async_computation | async-start | bytes 1572864 | tf_op jit(solution)/shard_map/all_to_all | solution.py:288
  19.7 178.1 %all-gather.4.cloned.1.call-start = ((), (), s32[]{:S(2)}) async-start(), calls=%async_computation.10 | async-start | bytes 2359296 | tf_op jit(solution)/shard_map/all_gather | solution.py:290
  21.3 47.6 %collective-permute-start.12 = (bf16[128,1024]{1,0:T(8,128)(2,1)}, bf16[128,1024]{1,0:T(8,128)(2,1)}, u32[]{:S(2)}, u32[]{:S(2)}) collective-permute-start(bf16[128,1024]{1,0:T(8,128)(2,1)} %get-tuple-element.126), channel_id=1, source_target_pairs={{0,8},{4,12},{8,0},{12,4},{16,24},{20,28},{24,16},{28,20},{1,9},{5... | collective-permute-start | bytes 786440 | tf_op jit(solution)/shard_map/ppermute | solution.py:38
  23.2 48.1 %collective-permute-start.15 = (bf16[128,1024]{1,0:T(8,128)(2,1)}, bf16[128,1024]{1,0:T(8,128)(2,1)S(1)}, u32[]{:S(2)}, u32[]{:S(2)}) collective-permute-start(bf16[128,1024]{1,0:T(8,128)(2,1)} %get-tuple-element.125), channel_id=1, source_target_pairs={{0,16},{4,20},{8,24},{12,28},{16,0},{20,4},{24,8},{28,12},{1,17},{... | collective-permute-start | bytes 786440 | tf_op jit(solution)/shard_map/ppermute | solution.py:38
  52.0 47.1 %all-to-all-start.4 = ((bf16[4,2,2,32,1024]{4,3,2,1,0:T(8,128)(2,1)}), bf16[4,2,2,32,1024]{4,3,2,1,0:T(8,128)(2,1)S(1)}, u32[]{:S(2)}, u32[]{:S(2)}) async-start(bf16[4,2,2,32,1024]{4,3,2,1,0:T(8,128)(2,1)} %bitcast.239), calls=%async_computation.4 | async-start | bytes 2097152 | tf_op jit(solution)/shard_map/all_to_all | solution.py:306
  65.2 15.1 %collective-permute-start.1 = (bf16[256,1024]{1,0:T(8,128)(2,1)}, bf16[256,1024]{1,0:T(8,128)(2,1)}, u32[]{:S(2)}, u32[]{:S(2)}) collective-permute-start(bf16[256,1024]{1,0:T(8,128)(2,1)} %pad_maximum_fusion.16), channel_id=1, source_target_pairs={{0,16},{4,20},{8,24},{12,28},{16,0},{20,4},{24,8},{28,12},{1,17},{... | collective-permute-start | bytes 1572872 | tf_op jit(solution)/shard_map/ppermute | solution.py:38
  67.3 15.2 %collective-permute-start.4 = (bf16[256,1024]{1,0:T(8,128)(2,1)}, bf16[256,1024]{1,0:T(8,128)(2,1)}, u32[]{:S(2)}, u32[]{:S(2)}) collective-permute-start(bf16[256,1024]{1,0:T(8,128)(2,1)} %pad_maximum_fusion.17), channel_id=1, source_target_pairs={{0,8},{4,12},{8,0},{12,4},{16,24},{20,28},{24,16},{28,20},{1,9},{5... | collective-permute-start | bytes 1572872 | tf_op jit(solution)/shard_map/ppermute | solution.py:38
  70.7 19.8 %collective-permute-start.13 = (bf16[256,1024]{1,0:T(8,128)(2,1)}, bf16[256,1024]{1,0:T(8,128)(2,1)}, u32[]{:S(2)}, u32[]{:S(2)}) collective-permute-start(bf16[256,1024]{1,0:T(8,128)(2,1)} %pad_maximum_fusion.20), channel_id=1, source_target_pairs={{0,16},{4,20},{8,24},{12,28},{16,0},{20,4},{24,8},{28,12},{1,17},{... | collective-permute-start | bytes 1572872 | tf_op jit(solution)/shard_map/ppermute | solution.py:38
  73.0 19.7 %collective-permute-start.16 = (bf16[256,1024]{1,0:T(8,128)(2,1)}, bf16[256,1024]{1,0:T(8,128)(2,1)}, u32[]{:S(2)}, u32[]{:S(2)}) collective-permute-start(bf16[256,1024]{1,0:T(8,128)(2,1)} %pad_maximum_fusion.21), channel_id=1, source_target_pairs={{0,8},{4,12},{8,0},{12,4},{16,24},{20,28},{24,16},{28,20},{1,9},{5... | collective-permute-start | bytes 1572872 | tf_op jit(solution)/shard_map/ppermute | solution.py:38
  82.5 19.2 %collective-permute-start.2 = (bf16[512,1024]{1,0:T(8,128)(2,1)}, bf16[512,1024]{1,0:T(8,128)(2,1)}, u32[]{:S(2)}, u32[]{:S(2)}) collective-permute-start(bf16[512,1024]{1,0:T(8,128)(2,1)} %pad_maximum_fusion.2), channel_id=1, source_target_pairs={{0,4},{4,0},{8,12},{12,8},{16,20},{20,16},{24,28},{28,24},{1,5},{5... | collective-permute-start | bytes 3145736 | tf_op jit(solution)/shard_map/ppermute | solution.py:38
  84.8 24.8 %collective-permute-start.5 = (bf16[512,1024]{1,0:T(8,128)(2,1)}, bf16[512,1024]{1,0:T(8,128)(2,1)}, u32[]{:S(2)}, u32[]{:S(2)}) collective-permute-start(bf16[512,1024]{1,0:T(8,128)(2,1)} %pad_maximum_fusion.3), channel_id=1, source_target_pairs={{0,4},{4,0},{8,12},{12,8},{16,20},{20,16},{24,28},{28,24},{1,5},{5... | collective-permute-start | bytes 3145736 | tf_op jit(solution)/shard_map/ppermute | solution.py:38
  92.7 66.9 %collective-permute-start.14 = (bf16[512,1024]{1,0:T(8,128)(2,1)}, bf16[512,1024]{1,0:T(8,128)(2,1)}, u32[]{:S(2)}, u32[]{:S(2)}) collective-permute-start(bf16[512,1024]{1,0:T(8,128)(2,1)} %pad_maximum_fusion.6), channel_id=1, source_target_pairs={{0,4},{4,0},{8,12},{12,8},{16,20},{20,16},{24,28},{28,24},{1,5},{5... | collective-permute-start | bytes 3145736 | tf_op jit(solution)/shard_map/ppermute | solution.py:38
  94.9 87.3 %collective-permute-start.17 = (bf16[512,1024]{1,0:T(8,128)(2,1)}, bf16[512,1024]{1,0:T(8,128)(2,1)}, u32[]{:S(2)}, u32[]{:S(2)}) collective-permute-start(bf16[512,1024]{1,0:T(8,128)(2,1)} %pad_maximum_fusion.7), channel_id=1, source_target_pairs={{0,4},{4,0},{8,12},{12,8},{16,20},{20,16},{24,28},{28,24},{1,5},{5... | collective-permute-start | bytes 3145736 | tf_op jit(solution)/shard_map/ppermute | solution.py:38
  100.2 40.5 %collective-permute-start.30 = (bf16[128,1024]{1,0:T(8,128)(2,1)S(1)}, bf16[128,1024]{1,0:T(8,128)(2,1)S(1)}, u32[]{:S(2)}, u32[]{:S(2)}) collective-permute-start(bf16[128,1024]{1,0:T(8,128)(2,1)S(1)} %get-tuple-element.112), channel_id=1, source_target_pairs={{0,8},{4,12},{8,0},{12,4},{16,24},{20,28},{24,16},{28,20},{1,9},{5... | collective-permute-start | bytes 786440 | tf_op jit(solution)/shard_map/ppermute | solution.py:38
  101.7 41.9 %collective-permute-start.48 = (bf16[128,1024]{1,0:T(8,128)(2,1)}, bf16[128,1024]{1,0:T(8,128)(2,1)S(1)}, u32[]{:S(2)}, u32[]{:S(2)}) collective-permute-start(bf16[128,1024]{1,0:T(8,128)(2,1)} %get-tuple-element.111), channel_id=1, source_target_pairs={{0,8},{4,12},{8,0},{12,4},{16,24},{20,28},{24,16},{28,20},{1,9},{5... | collective-permute-start | bytes 786440 | tf_op jit(solution)/shard_map/ppermute | solution.py:38
  109.5 35.2 %collective-permute-start.33 = (bf16[128,1024]{1,0:T(8,128)(2,1)}, bf16[128,1024]{1,0:T(8,128)(2,1)S(1)}, u32[]{:S(2)}, u32[]{:S(2)}) collective-permute-start(bf16[128,1024]{1,0:T(8,128)(2,1)} %get-tuple-element.109), channel_id=1, source_target_pairs={{0,16},{4,20},{8,24},{12,28},{16,0},{20,4},{24,8},{28,12},{1,17},{... | collective-permute-start | bytes 786440 | tf_op jit(solution)/shard_map/ppermute | solution.py:38
  136.2 48.3 %all-to-all-start.1 = ((bf16[8,2,128,128]{3,2,1,0:T(8,128)(2,1)}), bf16[8,2,128,128]{3,2,1,0:T(8,128)(2,1)}, u32[]{:S(2)}, u32[]{:S(2)}) async-start(bf16[8,2,128,128]{3,2,1,0:T(8,128)(2,1)} %attend.1), calls=%async_computation.1 | async-start | bytes 1048576 | tf_op jit(solution)/shard_map/all_to_all | solution.py:322
  143.7 23.1 %collective-permute-start.31 = (bf16[256,1024]{1,0:T(8,128)(2,1)S(1)}, bf16[256,1024]{1,0:T(8,128)(2,1)S(1)}, u32[]{:S(2)}, u32[]{:S(2)}) collective-permute-start(bf16[256,1024]{1,0:T(8,128)(2,1)S(1)} %pad_maximum_fusion.24), channel_id=1, source_target_pairs={{0,16},{4,20},{8,24},{12,28},{16,0},{20,4},{24,8},{28,12},{1,17},{... | collective-permute-start | bytes 1572872 | tf_op jit(solution)/shard_map/ppermute | solution.py:38
  144.8 32.6 %collective-permute-start.49 = (bf16[256,1024]{1,0:T(8,128)(2,1)S(1)}, bf16[256,1024]{1,0:T(8,128)(2,1)S(1)}, u32[]{:S(2)}, u32[]{:S(2)}) collective-permute-start(bf16[256,1024]{1,0:T(8,128)(2,1)S(1)} %pad_maximum_fusion.28), channel_id=1, source_target_pairs={{0,16},{4,20},{8,24},{12,28},{16,0},{20,4},{24,8},{28,12},{1,17},{... | collective-permute-start | bytes 1572872 | tf_op jit(solution)/shard_map/ppermute | solution.py:38
  155.5 30.4 %collective-permute-start.34 = (bf16[256,1024]{1,0:T(8,128)(2,1)}, bf16[256,1024]{1,0:T(8,128)(2,1)}, u32[]{:S(2)}, u32[]{:S(2)}) collective-permute-start(bf16[256,1024]{1,0:T(8,128)(2,1)} %pad_maximum_fusion.25), channel_id=1, source_target_pairs={{0,8},{4,12},{8,0},{12,4},{16,24},{20,28},{24,16},{28,20},{1,9},{5... | collective-permute-start | bytes 1572872 | tf_op jit(solution)/shard_map/ppermute | solution.py:38
  159.7 28.9 %collective-permute-start.52 = (bf16[256,1024]{1,0:T(8,128)(2,1)}, bf16[256,1024]{1,0:T(8,128)(2,1)}, u32[]{:S(2)}, u32[]{:S(2)}) collective-permute-start(bf16[256,1024]{1,0:T(8,128)(2,1)} %pad_maximum_fusion.29), channel_id=1, source_target_pairs={{0,8},{4,12},{8,0},{12,4},{16,24},{20,28},{24,16},{28,20},{1,9},{5... | collective-permute-start | bytes 1572872 | tf_op jit(solution)/shard_map/ppermute | solution.py:38
  167.9 24.5 %collective-permute-start.32 = (bf16[512,1024]{1,0:T(8,128)(2,1)}, bf16[512,1024]{1,0:T(8,128)(2,1)}, u32[]{:S(2)}, u32[]{:S(2)}) collective-permute-start(bf16[512,1024]{1,0:T(8,128)(2,1)} %pad_maximum_fusion.10), channel_id=1, source_target_pairs={{0,4},{4,0},{8,12},{12,8},{16,20},{20,16},{24,28},{28,24},{1,5},{5... | collective-permute-start | bytes 3145736 | tf_op jit(solution)/shard_map/ppermute | solution.py:38
  179.5 15.1 %collective-permute-start.50 = (bf16[512,1024]{1,0:T(8,128)(2,1)}, bf16[512,1024]{1,0:T(8,128)(2,1)}, u32[]{:S(2)}, u32[]{:S(2)}) collective-permute-start(bf16[512,1024]{1,0:T(8,128)(2,1)} %pad_maximum_fusion.14), channel_id=1, source_target_pairs={{0,4},{4,0},{8,12},{12,8},{16,20},{20,16},{24,28},{28,24},{1,5},{5... | collective-permute-start | bytes 3145736 | tf_op jit(solution)/shard_map/ppermute | solution.py:38
  188.1 25.6 %collective-permute-start.35 = (bf16[512,1024]{1,0:T(8,128)(2,1)}, bf16[512,1024]{1,0:T(8,128)(2,1)}, u32[]{:S(2)}, u32[]{:S(2)}) collective-permute-start(bf16[512,1024]{1,0:T(8,128)(2,1)} %pad_maximum_fusion.11), channel_id=1, source_target_pairs={{0,4},{4,0},{8,12},{12,8},{16,20},{20,16},{24,28},{28,24},{1,5},{5... | collective-permute-start | bytes 3145736 | tf_op jit(solution)/shard_map/ppermute | solution.py:38
  190.7 34.8 %collective-permute-start.53 = (bf16[512,1024]{1,0:T(8,128)(2,1)}, bf16[512,1024]{1,0:T(8,128)(2,1)}, u32[]{:S(2)}, u32[]{:S(2)}) collective-permute-start(bf16[512,1024]{1,0:T(8,128)(2,1)} %pad_maximum_fusion.15), channel_id=1, source_target_pairs={{0,4},{4,0},{8,12},{12,8},{16,20},{20,16},{24,28},{28,24},{1,5},{5... | collective-permute-start | bytes 3145736 | tf_op jit(solution)/shard_map/ppermute | solution.py:38
  202.4 32.1 %all-to-all-start.3 = ((bf16[4,2,2,32,1024]{4,3,2,1,0:T(8,128)(2,1)}), bf16[4,2,2,32,1024]{4,3,2,1,0:T(8,128)(2,1)}, u32[]{:S(2)}, u32[]{:S(2)}) async-start(bf16[4,2,2,32,1024]{4,3,2,1,0:T(8,128)(2,1)} %bitcast.266), calls=%async_computation.3 | async-start | bytes 2097152 | tf_op jit(solution)/shard_map/all_to_all | solution.py:306
  232.7 42.9 %collective-permute-start.11 = (bf16[512,1024]{1,0:T(8,128)(2,1)}, bf16[512,1024]{1,0:T(8,128)(2,1)}, u32[]{:S(2)}, u32[]{:S(2)}) collective-permute-start(bf16[512,1024]{1,0:T(8,128)(2,1)} %pad_maximum_fusion.5), channel_id=1, source_target_pairs={{0,4},{4,0},{8,12},{12,8},{16,20},{20,16},{24,28},{28,24},{1,5},{5... | collective-permute-start | bytes 3145736 | tf_op jit(solution)/shard_map/ppermute | solution.py:38
  234.5 34.9 %collective-permute-start.8 = (bf16[512,1024]{1,0:T(8,128)(2,1)}, bf16[512,1024]{1,0:T(8,128)(2,1)}, u32[]{:S(2)}, u32[]{:S(2)}) collective-permute-start(bf16[512,1024]{1,0:T(8,128)(2,1)} %pad_maximum_fusion.4), channel_id=1, source_target_pairs={{0,4},{4,0},{8,12},{12,8},{16,20},{20,16},{24,28},{28,24},{1,5},{5... | collective-permute-start | bytes 3145736 | tf_op jit(solution)/shard_map/ppermute | solution.py:38
  234.5 43.4 %all-to-all-start.2 = ((bf16[8,128,512]{2,1,0:T(8,128)(2,1)}), bf16[8,128,512]{2,1,0:T(8,128)(2,1)}, u32[]{:S(2)}, u32[]{:S(2)}) async-start(bf16[8,128,512]{2,1,0:T(8,128)(2,1)} %bitcast.264), calls=%async_computation.2 | async-start | bytes 2097152 | tf_op jit(solution)/shard_map/all_to_all | solution.py:293
  240.3 19.0 %collective-permute-start.42 = (bf16[128,1024]{1,0:T(8,128)(2,1)S(1)}, bf16[128,1024]{1,0:T(8,128)(2,1)S(1)}, u32[]{:S(2)}, u32[]{:S(2)}) collective-permute-start(bf16[128,1024]{1,0:T(8,128)(2,1)S(1)} %get-tuple-element.119), channel_id=1, source_target_pairs={{0,8},{4,12},{8,0},{12,4},{16,24},{20,28},{24,16},{28,20},{1,9},{5... | collective-permute-start | bytes 786440 | tf_op jit(solution)/shard_map/ppermute | solution.py:38
  243.1 21.3 %collective-permute-start.24 = (bf16[128,1024]{1,0:T(8,128)(2,1)S(1)}, bf16[128,1024]{1,0:T(8,128)(2,1)S(1)}, u32[]{:S(2)}, u32[]{:S(2)}) collective-permute-start(bf16[128,1024]{1,0:T(8,128)(2,1)S(1)} %get-tuple-element.120), channel_id=1, source_target_pairs={{0,8},{4,12},{8,0},{12,4},{16,24},{20,28},{24,16},{28,20},{1,9},{5... | collective-permute-start | bytes 786440 | tf_op jit(solution)/shard_map/ppermute | solution.py:38
  243.5 23.2 %collective-permute-start.27 = (bf16[128,1024]{1,0:T(8,128)(2,1)S(1)}, bf16[128,1024]{1,0:T(8,128)(2,1)S(1)}, u32[]{:S(2)}, u32[]{:S(2)}) collective-permute-start(bf16[128,1024]{1,0:T(8,128)(2,1)S(1)} %get-tuple-element.117), channel_id=1, source_target_pairs={{0,16},{4,20},{8,24},{12,28},{16,0},{20,4},{24,8},{28,12},{1,17},{... | collective-permute-start | bytes 786440 | tf_op jit(solution)/shard_map/ppermute | solution.py:38
  264.4 37.0 %collective-permute-start.43 = (bf16[256,1024]{1,0:T(8,128)(2,1)}, bf16[256,1024]{1,0:T(8,128)(2,1)}, u32[]{:S(2)}, u32[]{:S(2)}) collective-permute-start(bf16[256,1024]{1,0:T(8,128)(2,1)} %pad_maximum_fusion.26), channel_id=1, source_target_pairs={{0,16},{4,20},{8,24},{12,28},{16,0},{20,4},{24,8},{28,12},{1,17},{... | collective-permute-start | bytes 1572872 | tf_op jit(solution)/shard_map/ppermute | solution.py:38
  266.7 35.9 %collective-permute-start.25 = (bf16[256,1024]{1,0:T(8,128)(2,1)}, bf16[256,1024]{1,0:T(8,128)(2,1)}, u32[]{:S(2)}, u32[]{:S(2)}) collective-permute-start(bf16[256,1024]{1,0:T(8,128)(2,1)} %pad_maximum_fusion.22), channel_id=1, source_target_pairs={{0,16},{4,20},{8,24},{12,28},{16,0},{20,4},{24,8},{28,12},{1,17},{... | collective-permute-start | bytes 1572872 | tf_op jit(solution)/shard_map/ppermute | solution.py:38
  268.1 41.9 %collective-permute-start.28 = (bf16[256,1024]{1,0:T(8,128)(2,1)}, bf16[256,1024]{1,0:T(8,128)(2,1)}, u32[]{:S(2)}, u32[]{:S(2)}) collective-permute-start(bf16[256,1024]{1,0:T(8,128)(2,1)} %pad_maximum_fusion.23), channel_id=1, source_target_pairs={{0,8},{4,12},{8,0},{12,4},{16,24},{20,28},{24,16},{28,20},{1,9},{5... | collective-permute-start | bytes 1572872 | tf_op jit(solution)/shard_map/ppermute | solution.py:38
  269.4 45.3 %collective-permute-start.46 = (bf16[256,1024]{1,0:T(8,128)(2,1)}, bf16[256,1024]{1,0:T(8,128)(2,1)}, u32[]{:S(2)}, u32[]{:S(2)}) collective-permute-start(bf16[256,1024]{1,0:T(8,128)(2,1)} %pad_maximum_fusion.27), channel_id=1, source_target_pairs={{0,8},{4,12},{8,0},{12,4},{16,24},{20,28},{24,16},{28,20},{1,9},{5... | collective-permute-start | bytes 1572872 | tf_op jit(solution)/shard_map/ppermute | solution.py:38
  309.2 85.9 %collective-permute-start.18 = (bf16[512,2048]{1,0:T(8,128)(2,1)}, bf16[512,2048]{1,0:T(8,128)(2,1)}, u32[]{:S(2)}, u32[]{:S(2)}) collective-permute-start(bf16[512,2048]{1,0:T(8,128)(2,1)} %get-tuple-element.89), channel_id=1, source_target_pairs={{0,4},{4,0},{8,12},{12,8},{16,20},{20,16},{24,28},{28,24},{1,5},{5... | collective-permute-start | bytes 6291464 | tf_op jit(solution)/shard_map/ppermute | solution.py:38
  314.7 80.4 %collective-permute-start.21 = (bf16[512,2048]{1,0:T(8,128)(2,1)}, bf16[512,2048]{1,0:T(8,128)(2,1)}, u32[]{:S(2)}, u32[]{:S(2)}) collective-permute-start(bf16[512,2048]{1,0:T(8,128)(2,1)} %get-tuple-element.90), channel_id=1, source_target_pairs={{0,4},{4,0},{8,12},{12,8},{16,20},{20,16},{24,28},{28,24},{1,5},{5... | collective-permute-start | bytes 6291464 | tf_op jit(solution)/shard_map/ppermute | solution.py:38
  317.0 36.5 %collective-permute-start.47 = (bf16[512,1024]{1,0:T(8,128)(2,1)}, bf16[512,1024]{1,0:T(8,128)(2,1)}, u32[]{:S(2)}, u32[]{:S(2)}) collective-permute-start(bf16[512,1024]{1,0:T(8,128)(2,1)} %pad_maximum_fusion.13), channel_id=1, source_target_pairs={{0,4},{4,0},{8,12},{12,8},{16,20},{20,16},{24,28},{28,24},{1,5},{5... | collective-permute-start | bytes 3145736 | tf_op jit(solution)/shard_map/ppermute | solution.py:38
  350.4 33.7 %collective-permute-start.36 = (bf16[512,2048]{1,0:T(8,128)(2,1)S(1)}, bf16[512,2048]{1,0:T(8,128)(2,1)S(1)}, u32[]{:S(2)}, u32[]{:S(2)}) collective-permute-start(bf16[512,2048]{1,0:T(8,128)(2,1)S(1)} %get-tuple-element.93), channel_id=1, source_target_pairs={{0,4},{4,0},{8,12},{12,8},{16,20},{20,16},{24,28},{28,24},{1,5},{5... | collective-permute-start | bytes 6291464 | tf_op jit(solution)/shard_map/ppermute | solution.py:38
  350.5 37.2 %collective-permute-start.39 = (bf16[512,2048]{1,0:T(8,128)(2,1)}, bf16[512,2048]{1,0:T(8,128)(2,1)}, u32[]{:S(2)}, u32[]{:S(2)}) collective-permute-start(bf16[512,2048]{1,0:T(8,128)(2,1)} %get-tuple-element.94), channel_id=1, source_target_pairs={{0,4},{4,0},{8,12},{12,8},{16,20},{20,16},{24,28},{28,24},{1,5},{5... | collective-permute-start | bytes 6291464 | tf_op jit(solution)/shard_map/ppermute | solution.py:38
  384.0 21.6 %collective-permute-start.54 = (bf16[512,2048]{1,0:T(8,128)(2,1)}, bf16[512,2048]{1,0:T(8,128)(2,1)}, u32[]{:S(2)}, u32[]{:S(2)}) collective-permute-start(bf16[512,2048]{1,0:T(8,128)(2,1)} %get-tuple-element.97), channel_id=1, source_target_pairs={{0,4},{4,0},{8,12},{12,8},{16,20},{20,16},{24,28},{28,24},{1,5},{5... | collective-permute-start | bytes 6291464 | tf_op jit(solution)/shard_map/ppermute | solution.py:38
  384.1 21.5 %collective-permute-start.57 = (bf16[512,2048]{1,0:T(8,128)(2,1)}, bf16[512,2048]{1,0:T(8,128)(2,1)}, u32[]{:S(2)}, u32[]{:S(2)}) collective-permute-start(bf16[512,2048]{1,0:T(8,128)(2,1)} %get-tuple-element.98), channel_id=1, source_target_pairs={{0,4},{4,0},{8,12},{12,8},{16,20},{20,16},{24,28},{28,24},{1,5},{5... | collective-permute-start | bytes 6291464 | tf_op jit(solution)/shard_map/ppermute | solution.py:38
  393.5 26.1 %collective-permute-start.37 = (bf16[256,2048]{1,0:T(8,128)(2,1)S(1)}, bf16[256,2048]{1,0:T(8,128)(2,1)S(1)}, u32[]{:S(2)}, u32[]{:S(2)}) collective-permute-start(bf16[256,2048]{1,0:T(8,128)(2,1)S(1)} %slice.403), channel_id=1, source_target_pairs={{0,16},{4,20},{8,24},{12,28},{16,0},{20,4},{24,8},{28,12},{1,17},{... | collective-permute-start | bytes 3145736 | tf_op jit(solution)/shard_map/ppermute | solution.py:38
  404.1 91.0 %collective-permute-start.19 = (bf16[256,2048]{1,0:T(8,128)(2,1)}, bf16[256,2048]{1,0:T(8,128)(2,1)}, u32[]{:S(2)}, u32[]{:S(2)}) collective-permute-start(bf16[256,2048]{1,0:T(8,128)(2,1)} %slice.389), channel_id=1, source_target_pairs={{0,16},{4,20},{8,24},{12,28},{16,0},{20,4},{24,8},{28,12},{1,17},{... | collective-permute-start | bytes 3145736 | tf_op jit(solution)/shard_map/ppermute | solution.py:38
  405.3 26.2 %collective-permute-start.40 = (bf16[256,2048]{1,0:T(8,128)(2,1)}, bf16[256,2048]{1,0:T(8,128)(2,1)S(1)}, u32[]{:S(2)}, u32[]{:S(2)}) collective-permute-start(bf16[256,2048]{1,0:T(8,128)(2,1)} %slice.407), channel_id=1, source_target_pairs={{0,8},{4,12},{8,0},{12,4},{16,24},{20,28},{24,16},{28,20},{1,9},{5... | collective-permute-start | bytes 3145736 | tf_op jit(solution)/shard_map/ppermute | solution.py:38
  410.3 54.3 %collective-permute-start.55 = (bf16[256,2048]{1,0:T(8,128)(2,1)S(1)}, bf16[256,2048]{1,0:T(8,128)(2,1)S(1)}, u32[]{:S(2)}, u32[]{:S(2)}) collective-permute-start(bf16[256,2048]{1,0:T(8,128)(2,1)S(1)} %slice.415), channel_id=1, source_target_pairs={{0,16},{4,20},{8,24},{12,28},{16,0},{20,4},{24,8},{28,12},{1,17},{... | collective-permute-start | bytes 3145736 | tf_op jit(solution)/shard_map/ppermute | solution.py:38
  412.4 53.1 %collective-permute-start.58 = (bf16[256,2048]{1,0:T(8,128)(2,1)S(1)}, bf16[256,2048]{1,0:T(8,128)(2,1)S(1)}, u32[]{:S(2)}, u32[]{:S(2)}) collective-permute-start(bf16[256,2048]{1,0:T(8,128)(2,1)S(1)} %slice.419), channel_id=1, source_target_pairs={{0,8},{4,12},{8,0},{12,4},{16,24},{20,28},{24,16},{28,20},{1,9},{5... | collective-permute-start | bytes 3145736 | tf_op jit(solution)/shard_map/ppermute | solution.py:38
  420.1 47.6 %collective-permute-start.38 = (bf16[128,2048]{1,0:T(8,128)(2,1)S(1)}, bf16[128,2048]{1,0:T(8,128)(2,1)S(1)}, u32[]{:S(2)}, u32[]{:S(2)}) collective-permute-start(bf16[128,2048]{1,0:T(8,128)(2,1)S(1)} %slice.405), channel_id=1, source_target_pairs={{0,8},{4,12},{8,0},{12,4},{16,24},{20,28},{24,16},{28,20},{1,9},{5... | collective-permute-start | bytes 1572872 | tf_op jit(solution)/shard_map/ppermute | solution.py:38
  432.0 43.8 %collective-permute-start.41 = (bf16[128,2048]{1,0:T(8,128)(2,1)S(1)}, bf16[128,2048]{1,0:T(8,128)(2,1)S(1)}, u32[]{:S(2)}, u32[]{:S(2)}) collective-permute-start(bf16[128,2048]{1,0:T(8,128)(2,1)S(1)} %slice.409), channel_id=1, source_target_pairs={{0,16},{4,20},{8,24},{12,28},{16,0},{20,4},{24,8},{28,12},{1,17},{... | collective-permute-start | bytes 1572872 | tf_op jit(solution)/shard_map/ppermute | solution.py:38
  465.9 20.6 %collective-permute-start.59 = (bf16[128,2048]{1,0:T(8,128)(2,1)S(1)}, bf16[128,2048]{1,0:T(8,128)(2,1)S(1)}, u32[]{:S(2)}, u32[]{:S(2)}) collective-permute-start(bf16[128,2048]{1,0:T(8,128)(2,1)S(1)} %slice.421), channel_id=1, source_target_pairs={{0,16},{4,20},{8,24},{12,28},{16,0},{20,4},{24,8},{28,12},{1,17},{... | collective-permute-start | bytes 1572872 | tf_op jit(solution)/shard_map/ppermute | solution.py:38
  488.1 52.9 %all-to-all-start.5 = ((bf16[4,2,2,32,2048]{4,3,2,1,0:T(8,128)(2,1)}), bf16[4,2,2,32,2048]{4,3,2,1,0:T(8,128)(2,1)}, u32[]{:S(2)}, u32[]{:S(2)}) async-start(bf16[4,2,2,32,2048]{4,3,2,1,0:T(8,128)(2,1)} %maximum_bitcast_fusion), calls=%async_computation.5 | async-start | bytes 4194304 | tf_op jit(solution)/shard_map/all_to_all | solution.py:351
  494.6 26.1 %collective-permute-start.22 = (bf16[256,2048]{1,0:T(8,128)(2,1)S(1)}, bf16[256,2048]{1,0:T(8,128)(2,1)S(1)}, u32[]{:S(2)}, u32[]{:S(2)}) collective-permute-start(bf16[256,2048]{1,0:T(8,128)(2,1)S(1)} %slice.393), channel_id=1, source_target_pairs={{0,8},{4,12},{8,0},{12,4},{16,24},{20,28},{24,16},{28,20},{1,9},{5... | collective-permute-start | bytes 3145736 | tf_op jit(solution)/shard_map/ppermute | solution.py:38
  497.1 33.3 %collective-permute-start.20 = (bf16[128,2048]{1,0:T(8,128)(2,1)S(1)}, bf16[128,2048]{1,0:T(8,128)(2,1)S(1)}, u32[]{:S(2)}, u32[]{:S(2)}) collective-permute-start(bf16[128,2048]{1,0:T(8,128)(2,1)S(1)} %slice.391), channel_id=1, source_target_pairs={{0,8},{4,12},{8,0},{12,4},{16,24},{20,28},{24,16},{28,20},{1,9},{5... | collective-permute-start | bytes 1572872 | tf_op jit(solution)/shard_map/ppermute | solution.py:38
  552.9 82.1 %reduce-scatter.2.cloned.1.call-start = ((), (), s32[]{:S(2)}) async-start(), calls=%async_computation.11 | async-start | bytes 2654208 | tf_op jit(solution)/shard_map/reduce_scatter | solution.py:386
  562.6 33.4 %all-to-all-start.8 = ((bf16[8,128,512]{2,1,0:T(8,128)(2,1)}), bf16[8,128,512]{2,1,0:T(8,128)(2,1)S(1)}, u32[]{:S(2)}, u32[]{:S(2)}) async-start(bf16[8,128,512]{2,1,0:T(8,128)(2,1)} %bitcast.93), calls=%async_computation.9 | async-start | bytes 2097152 | tf_op jit(solution)/shard_map/all_to_all | solution.py:339
  594.1 20.2 %collective-permute-start.60 = (bf16[512,1024]{1,0:T(8,128)(2,1)}, bf16[512,1024]{1,0:T(8,128)(2,1)}, u32[]{:S(2)}, u32[]{:S(2)}) collective-permute-start(bf16[512,1024]{1,0:T(8,128)(2,1)} %get-tuple-element.102), channel_id=1, source_target_pairs={{0,4},{4,0},{8,12},{12,8},{16,20},{20,16},{24,28},{28,24},{1,5},{5... | collective-permute-start | bytes 3145736 | tf_op jit(solution)/shard_map/ppermute | solution.py:38
  594.6 19.7 %collective-permute-start.63 = (bf16[512,1024]{1,0:T(8,128)(2,1)}, bf16[512,1024]{1,0:T(8,128)(2,1)}, u32[]{:S(2)}, u32[]{:S(2)}) collective-permute-start(bf16[512,1024]{1,0:T(8,128)(2,1)} %get-tuple-element.103), channel_id=1, source_target_pairs={{0,4},{4,0},{8,12},{12,8},{16,20},{20,16},{24,28},{28,24},{1,5},{5... | collective-permute-start | bytes 3145736 | tf_op jit(solution)/shard_map/ppermute | solution.py:38
  609.6 18.9 %all-to-all-start.7 = ((bf16[8,144,384]{2,1,0:T(8,128)(2,1)}), bf16[8,144,384]{2,1,0:T(8,128)(2,1)}, u32[]{:S(2)}, u32[]{:S(2)}) async-start(bf16[8,144,384]{2,1,0:T(8,128)(2,1)} %fusion.19), calls=%async_computation.8 | async-start | bytes 1769472 | tf_op jit(solution)/shard_map/all_to_all | solution.py:399
  613.9 141.7 %all-reduce.6.cloned.1.call-start = ((), (), s32[]{:S(2)}) async-start(), calls=%async_computation.12 | async-start | bytes 6291456 | tf_op jit(solution)/shard_map/psum | solution.py:404
  619.3 18.5 %collective-permute-start.61 = (bf16[256,1024]{1,0:T(8,128)(2,1)}, bf16[256,1024]{1,0:T(8,128)(2,1)}, u32[]{:S(2)}, u32[]{:S(2)}) collective-permute-start(bf16[256,1024]{1,0:T(8,128)(2,1)} %slice.428), channel_id=1, source_target_pairs={{0,16},{4,20},{8,24},{12,28},{16,0},{20,4},{24,8},{28,12},{1,17},{... | collective-permute-start | bytes 1572872 | tf_op jit(solution)/shard_map/ppermute | solution.py:38
  624.6 16.2 %collective-permute-start.64 = (bf16[256,1024]{1,0:T(8,128)(2,1)}, bf16[256,1024]{1,0:T(8,128)(2,1)}, u32[]{:S(2)}, u32[]{:S(2)}) collective-permute-start(bf16[256,1024]{1,0:T(8,128)(2,1)} %slice.434), channel_id=1, source_target_pairs={{0,8},{4,12},{8,0},{12,4},{16,24},{20,28},{24,16},{28,20},{1,9},{5... | collective-permute-start | bytes 1572872 | tf_op jit(solution)/shard_map/ppermute | solution.py:38
  (75 other events, 983.7 us)
Sparse Core Ops, SparseCore 0:
  22.4 32.2 all-gather.3
  557.0 41.7 reduce-scatter.1
  636.8 118.6 all-reduce.5
